TPU v7x, 32 devices: a whole 2x2x4 slice. The times are simulated.
32 devices in a mesh: seq: 8 (over z, y), head: 4 (over x, core).
Axes of the slice: x: 2, y: 2, z: 4, core: 2. Of those that a mesh axis runs over, the one named last changes fastest.
Arguments:
- queries: bfloat16 [8192, 2048], P(('seq', 'head')), may hold values from -0.1875 to 0.1875
- key_rows: bfloat16 [8192, 2048], P(('seq', 'head')), may hold values from -1 to 1
- value_matrix: bfloat16 [8192, 2048], P(('seq', 'head')), may hold values from -1.75 to 1.75
- log_decay: bfloat16 [8192, 2048], P(('seq', 'head')), may hold values from -1 to 0, as said below
- beta_gate: bfloat16 [8192, 16], P(('seq', 'head')), may hold values from 0.19921875 to 1
- grad_out: bfloat16 [8192, 2048], P(('seq', 'head')), may hold values from -6 to 6
Outputs:
- grad_queries: bfloat16 [8192, 2048], P(('seq', 'head'))
- grad_keys: bfloat16 [8192, 2048], P(('seq', 'head'))
- grad_values: bfloat16 [8192, 2048], P(('seq', 'head'))
- grad_decay: bfloat16 [8192, 2048], P(('seq', 'head'))
- grad_beta: bfloat16 [8192, 16], P(('seq', 'head'))
Inputs may be any that keep to these rules, and one draw needn't show every extreme that they name: `log_decay`: log decays are negative.
All inputs are finite; a program needn't handle non-finite values.
Results may differ from a plain program's by a relative error of at most 0.0095.
Values may be sent and summed in bfloat16 or wider, within the bound.
No kernel may reach another device: no remote copies, remote signals or barrier semaphores. Data moves between devices by JAX's collectives and lax.ppermute only.
A program may use at most 256 MiB of HBM per device.

v0:
```python
import jax
import jax.numpy as jnp
from jax import lax
from jax.sharding import PartitionSpec as P

DK = 128
DV = 128
SPAN = 64


PRECISE = lax.Precision.HIGHEST


def entering(shard, axis, join, neutral, backward):
    count = lax.axis_size(axis)
    place = lax.axis_index(axis)
    ahead = count - 1 - place if backward else place
    gathered = jax.tree.map(
        lambda a, kind: lax.all_gather(a.astype(kind), axis), shard, (jnp.bfloat16, jnp.bfloat16)
    )
    state = jax.tree.map(lambda a, e: jnp.zeros_like(a) + jnp.asarray(e, a.dtype), shard, neutral)

    def one(turn, state):
        source = count - 1 - turn if backward else turn
        return join(
            state,
            jax.tree.map(
                lambda a, own: lax.dynamic_index_in_dim(a, source, 0, False).astype(own.dtype),
                gathered,
                shard,
            ),
        )

    return lax.fori_loop(0, ahead, one, state)


def matrix_product(form, left, right):
    return jnp.einsum(form, left, right, precision=PRECISE)


def substitute(system):
    order_size = system.shape[-1]
    leading = system.shape[:-2]
    flattened = system.reshape((-1, order_size, order_size)).transpose(1, 2, 0)
    identity = jnp.eye(order_size, dtype=jnp.float32)
    found_rows = []
    for row_index in range(order_size):
        current = jnp.broadcast_to(identity[row_index][:, None], (order_size, flattened.shape[2]))
        if row_index > 0:
            earlier_rows = jnp.stack(found_rows)
            current = current - jnp.sum(
                flattened[row_index, :row_index][:, None, :] * earlier_rows, axis=0
            )
        found_rows.append(current)
    return jnp.stack(found_rows).transpose(2, 0, 1).reshape(leading + (order_size, order_size))


def unit_lower_inverse(system):
    order_size = system.shape[-1]
    if order_size <= 16:
        return substitute(system)
    half_size = order_size // 2
    blocks = unit_lower_inverse(
        jnp.stack([system[..., :half_size, :half_size], system[..., half_size:, half_size:]])
    )
    upper_block = blocks[0]
    lower_block = blocks[1]
    corner = -matrix_product(
        "...ij,...jk->...ik",
        lower_block,
        matrix_product("...ij,...jk->...ik", system[..., half_size:, :half_size], upper_block),
    )
    top_rows = jnp.concatenate([upper_block, jnp.zeros_like(upper_block)], axis=-1)
    bottom_rows = jnp.concatenate([corner, lower_block], axis=-1)
    return jnp.concatenate([top_rows, bottom_rows], axis=-2)


def span_tables(queries, key_rows, decays, betas):
    length = decays.shape[-2]
    running = jnp.cumsum(decays, axis=-2)
    middle = running[..., length // 2 : length // 2 + 1, :]
    ending = running[..., length - 1 :, :]
    key_up = key_rows * jnp.exp(running - middle)
    key_down = key_rows * jnp.exp(middle - running)
    query_up = queries * jnp.exp(running - middle)
    row_ids = lax.broadcasted_iota(jnp.int32, (length, length), 0)
    col_ids = lax.broadcasted_iota(jnp.int32, (length, length), 1)
    key_pairs = matrix_product("...cd,...sd->...cs", key_up, key_down)
    scores = matrix_product("...cd,...sd->...cs", query_up, key_down)
    linear_system = jnp.where(row_ids > col_ids, key_pairs, 0.0) * betas[..., None, :] + jnp.eye(
        length, dtype=jnp.float32
    )
    reachability_table = jnp.where(row_ids >= col_ids, scores, 0.0) * betas[..., None, :]
    key_offset = key_rows * jnp.exp(running)
    query_offset = queries * jnp.exp(running)
    last_key = key_rows * jnp.exp(ending - running) * betas[..., :, None]
    return (
        unit_lower_inverse(linear_system),
        reachability_table,
        key_offset,
        query_offset,
        last_key,
        jnp.exp(ending[..., 0, :]),
    )


def span_apply(carried_state, pieces):
    queries, key_rows, value_matrix, decays, betas = pieces
    inverse, reachability_table, key_offset, query_offset, last_key, final_decay = span_tables(
        queries, key_rows, decays, betas
    )
    written_state = matrix_product(
        "...cs,...sv->...cv",
        inverse,
        value_matrix - matrix_product("...cm,...mv->...cv", key_offset, carried_state),
    )
    output_rows = matrix_product(
        "...cm,...mv->...cv", query_offset, carried_state
    ) + matrix_product("...cs,...sv->...cv", reachability_table, written_state)
    carried_state = final_decay[..., :, None] * carried_state + matrix_product(
        "...ck,...cv->...kv", last_key, written_state
    )
    return (carried_state, output_rows)


def compose(earlier, later):
    return (
        matrix_product("hij,hjk->hik", later[0], earlier[0]),
        matrix_product("hij,hjk->hik", later[0], earlier[1]) + later[1],
    )


def reduce_maps(maps, reads):
    levels = []
    while maps.shape[0] > 1:
        levels.append(maps)
        count = maps.shape[0]
        paired = count // 2 * 2
        early_maps = maps[0:paired:2]
        late_maps = maps[1:paired:2]
        merged_maps = matrix_product("nhij,nhjk->nhik", late_maps, early_maps)
        merged_reads = reads[0:paired:2] + matrix_product(
            "nhji,nhjv->nhiv", early_maps, reads[1:paired:2]
        )
        maps = merged_maps
        reads = merged_reads
    return (levels, maps[0], reads[0])


def reduce_shifts(levels, shifts):
    for maps in levels:
        count = maps.shape[0]
        paired = count // 2 * 2
        merged = (
            matrix_product("nhij,nhjv->nhiv", maps[1:paired:2], shifts[0:paired:2])
            + shifts[1:paired:2]
        )
        shifts = merged
    return shifts[0]


def local(queries, key_rows, value_matrix, log_decay, beta_gate, grad_out):
    query_block, key_block, grad_block, decay_block, beta_block, value_block = (
        lax.all_to_all(queries, "head", split_axis=1, concat_axis=0, tiled=True),
        lax.all_to_all(key_rows, "head", split_axis=1, concat_axis=0, tiled=True),
        lax.all_to_all(grad_out, "head", split_axis=1, concat_axis=0, tiled=True),
        lax.all_to_all(log_decay, "head", split_axis=1, concat_axis=0, tiled=True),
        lax.all_to_all(beta_gate, "head", split_axis=1, concat_axis=0, tiled=True),
        lax.all_to_all(value_matrix, "head", split_axis=1, concat_axis=0, tiled=True),
    )
    heads = beta_block.shape[1]
    spans = beta_block.shape[0] // SPAN

    def arrange(source):
        return (
            source.astype(jnp.float32)
            .reshape(spans, SPAN, heads, source.shape[1] // heads)
            .transpose(0, 2, 1, 3)
        )

    query_parts = arrange(query_block)
    key_parts = arrange(key_block)
    decay_parts = arrange(decay_block)
    grad_parts = arrange(grad_block)
    beta_parts = beta_block.astype(jnp.float32).reshape(spans, SPAN, heads).transpose(0, 2, 1)
    identity_stack = jnp.broadcast_to(jnp.eye(DK, dtype=jnp.float32), (heads, DK, DK))
    zero_state = jnp.zeros((heads, DK, DV), jnp.float32)
    inverse, reach_tables, key_offsets, query_offsets, key_ends, final_decays = span_tables(
        query_parts, key_parts, decay_parts, beta_parts
    )
    across = matrix_product("nhcs,nhsk->nhck", inverse, key_offsets)
    transits = final_decays[..., :, None] * jnp.eye(DK, dtype=jnp.float32) - matrix_product(
        "nhck,nhcj->nhkj", key_ends, across
    )
    readouts = query_offsets - matrix_product("nhcs,nhsk->nhck", reach_tables, across)
    read_terms = matrix_product("nhck,nhcv->nhkv", readouts, grad_parts)
    levels, block_map, block_read = reduce_maps(transits, read_terms)
    later_maps = entering(
        (jnp.swapaxes(block_map, 1, 2), block_read),
        "seq",
        compose,
        (identity_stack, zero_state),
        True,
    )
    value_parts = arrange(value_block)
    write_terms = matrix_product(
        "nhck,nhcv->nhkv", key_ends, matrix_product("nhcs,nhsv->nhcv", inverse, value_parts)
    )
    block_shift = reduce_shifts(levels, write_terms)
    earlier_maps = entering(
        (block_map, block_shift), "seq", compose, (identity_stack, zero_state), False
    )
    start_state = earlier_maps[1]
    end_grad = later_maps[1]

    def chain_step(carried, members):
        forward_state, backward_grad = carried
        forward_map, forward_shift, backward_map, backward_read = members
        next_state = matrix_product("hij,hjv->hiv", forward_map, forward_state) + forward_shift
        next_grad = matrix_product("hji,hjv->hiv", backward_map, backward_grad) + backward_read
        return ((next_state, next_grad), (forward_state, backward_grad))

    _, (span_starts, reversed_grads) = lax.scan(
        chain_step,
        (start_state, end_grad),
        (transits, write_terms, transits[::-1], read_terms[::-1]),
    )
    span_ends = reversed_grads[::-1]

    def span_gradients(
        start_entry,
        query_entry,
        key_entry,
        value_entry,
        decay_entry,
        beta_entry,
        grad_entry,
        end_entry,
    ):

        def forward(query_input, key_input, value_input, decay_input, beta_input):
            return span_apply(
                start_entry, (query_input, key_input, value_input, decay_input, beta_input)
            )

        _, pull_back = jax.vjp(
            forward, query_entry, key_entry, value_entry, decay_entry, beta_entry
        )
        return pull_back((end_entry, grad_entry))

    grad_query, grad_key, grad_value, grad_decay, grad_gate = jax.vmap(span_gradients)(
        span_starts,
        query_parts,
        key_parts,
        value_parts,
        decay_parts,
        beta_parts,
        grad_parts,
        span_ends,
    )

    def restore(source):
        return (
            source.transpose(0, 2, 1, 3)
            .reshape(spans * SPAN, heads * source.shape[3])
            .astype(jnp.bfloat16)
        )

    gate_rows = grad_gate.transpose(0, 2, 1).reshape(spans * SPAN, heads).astype(jnp.bfloat16)
    return (
        lax.all_to_all(restore(grad_query), "head", split_axis=0, concat_axis=1, tiled=True),
        lax.all_to_all(restore(grad_key), "head", split_axis=0, concat_axis=1, tiled=True),
        lax.all_to_all(restore(grad_value), "head", split_axis=0, concat_axis=1, tiled=True),
        lax.all_to_all(restore(grad_decay), "head", split_axis=0, concat_axis=1, tiled=True),
        lax.all_to_all(gate_rows, "head", split_axis=0, concat_axis=1, tiled=True),
    )


def solution(mesh):
    return jax.shard_map(
        local,
        mesh=mesh,
        in_specs=(
            P(("seq", "head"), None),
            P(("seq", "head"), None),
            P(("seq", "head"), None),
            P(("seq", "head"), None),
            P(("seq", "head"), None),
            P(("seq", "head"), None),
        ),
        out_specs=(
            P(("seq", "head"), None),
            P(("seq", "head"), None),
            P(("seq", "head"), None),
            P(("seq", "head"), None),
            P(("seq", "head"), None),
        ),
        check_vma=False,
    )
```

profile of v0, /device:TPU:0, one launch (start us, length us, event | category | flops | bytes accessed | tf_op | source)
XLA Modules:
  0.0 688.5 jit_solution(14987350845251507145)
XLA Ops:
  25.9 11.7 %all-to-all-done = bf16[256,4,512]{2,0,1:T(8,128)(2,1)S(1)} async-done(((bf16[256,4,512]{2,0,1:T(8,128)(2,1)}), bf16[256,4,512]{2,0,1:T(8,128)(2,1)S(1)}, u32[]{:S(2)}, u32[]{:S(2)}) %all-to-all-start) | async-done | bytes 1048608 | tf_op jit(solution)/shard_map/all_to_all | solution.py:167
  45.6 10.7 %all-to-all-done.1 = bf16[256,4,512]{2,0,1:T(8,128)(2,1)} async-done(((bf16[256,4,512]{2,0,1:T(8,128)(2,1)}), bf16[256,4,512]{2,0,1:T(8,128)(2,1)}, u32[]{:S(2)}, u32[]{:S(2)}) %all-to-all-start.1) | async-done | bytes 1048608 | tf_op jit(solution)/shard_map/all_to_all | solution.py:165
  66.5 9.7 %multiply_add_fusion = (f32[16,4,64,64]{3,2,1,0:T(8,128)S(1)}, f32[16,4,64,64]{3,2,1,0:T(8,128)}) fusion(f32[64,64]{1,0:T(8,128)S(1)} %fusion.186, f32[16,4,64]{2,1,0:T(4,128)S(1)} %copy.193, pred[64,64]{1,0:T(8,128)(4,1)S(1)} %iota_compare_fusion.6, f32[16,64,4,128]{3,2,1,0:T(4,128)} %reshape.1062, f32[16,4,128]{2,1,0:T(4,128)S(1)} %copy.194, ...), kind=kOutput, calls=%fused_computation.114 | convolution fusion | flops 405536768 | bytes 6361088 | tf_op jit(solution)/shard_map/...cd,...sd->...cs/dot_general | solution.py:38
  126.4 8.9 %fusion.160 = f32[16,4,64,64]{3,2,1,0:T(8,128)} fusion(f32[16,64,4,128]{3,2,1,0:T(4,128)} %reshape.1063, f32[16,4,128]{2,1,0:T(4,128)S(1)} %copy.194, f32[16,4,64,128]{3,0,1,2:T(8,128)S(1)} %fusion.35, f32[16,64,4,128]{3,2,1,0:T(4,128)S(1)} %copy-done.1), kind=kOutput, calls=%fused_computation.273 | convolution fusion | flops 404750336 | bytes 7372800 | tf_op jit(solution)/shard_map/...cd,...sd->...cs/dot_general | solution.py:38
  141.2 6.5 fusion.152
  147.7 8.8 %multiply_subtract_fusion = f32[16,4,128,128]{3,2,1,0:T(8,128)S(1)} fusion(f32[16,4,64,128]{3,2,1,0:T(8,128)S(1)} %fusion.152, f32[128,128]{1,0:T(8,128)S(1)} %fusion.183, f32[16,4,128]{2,1,0:T(4,128)S(1)} %exp.45, f32[16,4,64,128]{3,2,1,0:T(8,128)S(1)} %copy-done.5, f32[16,4,64]{2,1,0:T(4,128)S(1)} %copy.193), kind=kOutput, calls=%fused_computation.19 | convolution fusion | flops 807927808 | bytes 8503296 | tf_op jit(solution)/shard_map/nhck,nhcj->nhkj/dot_general | solution.py:38
  225.7 5.8 stack.102
  234.3 5.9 stack.103
  243.1 6.1 stack.104
  253.2 7.3 %fusion.70 = f32[16,4,128,128]{3,2,1,0:T(8,128)S(1)} fusion(f32[16,4,64,128]{3,2,1,0:T(8,128)S(1)} %fusion.106, f32[16,4,64,128]{3,2,1,0:T(8,128)S(1)} %copy-done.6, f32[16,4,64]{2,1,0:T(4,128)S(1)} %copy.193), kind=kOutput, calls=%fused_computation.135 | convolution fusion | flops 805830656 | bytes 8404992 | tf_op jit(solution)/shard_map/nhck,nhcv->nhkv/dot_general | solution.py:38
  286.7 6.1 stack.105
  295.7 6.3 stack.106
  304.9 6.4 stack.107
  326.3 9.2 %while.43 = (s32[]{:T(128)}, f32[4,128,128]{2,1,0:T(8,128)S(1)}, s32[]{:T(128)}, bf16[8,4,128,128]{3,2,1,0:T(8,128)(2,1)}, bf16[8,4,128,128]{3,2,1,0:T(8,128)(2,...) while((s32[]{:T(128)}, f32[4,128,128]{2,1,0:T(8,128)S(1)}, s32[]{:T(128)}, ...), condition=%wide.region_18.19_spmd, body=%wide.region_17.18_spmd.sunk | while | flops 100794376 | bytes 1311883 | solution.py:34
  335.6 38.3 %all-gather.11.cloned.1.call-done = bf16[32,128,128]{2,1,0:T(8,128)(2,1)} async-done(((bf16[4,128,128]{2,1,0:T(8,128)(2,1)}), bf16[32,128,128]{2,1,0:T(8,128)(2,1)}) %all-gather.11.cloned.1.call-update) | async-done | bytes 1048592 | tf_op jit(solution)/shard_map/all_gather | solution.py:19
  373.9 64.0 %while.44 = (s32[]{:T(128)}, f32[4,128,128]{2,1,0:T(8,128)S(1)}, f32[4,128,128]{2,1,0:T(8,128)S(1)}, f32[16,4,128,128]{3,2,1,0:T(8,128)}, f32[16,4,128,128]{3,2,...) while((s32[]{:T(128)}, f32[4,128,128]{2,1,0:T(8,128)S(1)}, ...), condition=%wide.region_20.21_spmd, body=%wide.region_19.20_spmd.sunk | while | flops 201457664 | bytes 4196965 | solution.py:223
  438.0 6.9 fusion.68
  522.8 6.5 fusion.61
  538.3 8.2 %fusion.222 = f32[16,4,64,128]{3,2,1,0:T(8,128)S(1)} fusion(f32[16,4,64,128]{3,2,1,0:T(8,128)S(1)} %fusion.154, f32[16,4,128,128]{3,2,1,0:T(8,128)S(1)} %copy-done.15), kind=kOutput, calls=%fused_computation.669 | convolution fusion | flops 805306368 | bytes 8388608 | tf_op jit(solution)/shard_map/vmap(transpose(jvp(...ck,...cv->...kv)))/dot_general | solution.py:38
  565.1 10.6 %fusion.85 = (f32[16,4,128]{2,1,0:T(4,128)S(1)}, f32[16,4,128]{2,1,0:T(4,128)S(1)}, f32[16,4,128]{2,1,0:T(4,128)S(1)}, f32[16,4,128]{2,1,0:T(4,128)S(1)}, f32[16...) fusion(f32[16,64,4,128]{3,2,1,0:T(4,128)S(1)} %copy-done.3, f32[16,4,128]{2,1,0:T(4,128)S(1)} %copy.194, ...), kind=kOutput, calls=%fused_computation.158 | convolution fusion | flops 414150656 | bytes 20156416 | tf_op jit(solution)/shard_map/vmap(transpose(jvp(...cd,...sd->...cs)))/dot_general | solution.py:38
  581.0 16.6 %fusion.20 = (bf16[16,64,4,128]{3,1,2,0:T(8,128)(2,1)S(1)}, bf16[16,64,4,128]{3,1,2,0:T(8,128)(2,1)}, f32[16,4,64,128]{3,2,1,0:T(8,128)S(1)}) fusion(f32[16,4,64,128]{3,2,1,0:T(8,128)} %copy-done.21, f32[16,4,64,128]{3,2,1,0:T(8,128)} %copy-done.25, f32[16,4,64,128]{3,2,1,0:T(8,128)} %get-tuple-element.485, f32[16,64,4]{1,2,0:T(4,128)S(1)} %copy-done.130, ...), kind=kOutput, calls=%fused_computation.46 | convolution fusion | flops 814219264 | bytes 23150592 | tf_op jit(solution)/shard_map/vmap(transpose(jvp(...cm,...mv->...cv)))/dot_general | solution.py:38
  614.7 10.3 %all-to-all-done.9 = bf16[4,256,512]{2,1,0:T(8,128)(2,1)S(1)} async-done(((bf16[4,256,512]{2,1,0:T(8,128)(2,1)}), bf16[4,256,512]{2,1,0:T(8,128)(2,1)S(1)}, u32[]{:S(2)}, u32[]{:S(2)}) %all-to-all-start.9) | async-done | bytes 1048608 | tf_op jit(solution)/shard_map/all_to_all | solution.py:274
  633.6 10.3 %all-to-all-done.6 = bf16[4,256,512]{2,1,0:T(8,128)(2,1)} async-done(((bf16[4,256,512]{2,1,0:T(8,128)(2,1)}), bf16[4,256,512]{2,1,0:T(8,128)(2,1)}, u32[]{:S(2)}, u32[]{:S(2)}) %all-to-all-start.6) | async-done | bytes 1048608 | tf_op jit(solution)/shard_map/all_to_all | solution.py:271
  649.7 12.1 %all-to-all-done.7 = bf16[4,256,512]{2,1,0:T(8,128)(2,1)S(1)} async-done(((bf16[4,256,512]{2,1,0:T(8,128)(2,1)}), bf16[4,256,512]{2,1,0:T(8,128)(2,1)S(1)}, u32[]{:S(2)}, u32[]{:S(2)}) %all-to-all-start.7) | async-done | bytes 1048608 | tf_op jit(solution)/shard_map/all_to_all | solution.py:272
  (705 shorter events, 450.1 us)
Async XLA Ops:
  8.6 11.0 %all-to-all-start.2 = ((bf16[256,4,4]{0,2,1:T(4,128)(2,1)}), bf16[256,4,4]{0,2,1:T(4,128)(2,1)S(1)}, u32[]{:S(2)}, u32[]{:S(2)}) async-start(bf16[256,4,4]{0,2,1:T(4,128)(2,1)} %all_to_all.128), calls=%async_computation.2 | async-start | bytes 16384 | tf_op jit(solution)/shard_map/all_to_all | solution.py:168
  19.6 18.0 %all-to-all-start = ((bf16[256,4,512]{2,0,1:T(8,128)(2,1)}), bf16[256,4,512]{2,0,1:T(8,128)(2,1)S(1)}, u32[]{:S(2)}, u32[]{:S(2)}) async-start(bf16[256,4,512]{2,0,1:T(8,128)(2,1)} %bitcast.659), calls=%async_computation | async-start | bytes 2097152 | tf_op jit(solution)/shard_map/all_to_all | solution.py:167
  37.6 18.8 %all-to-all-start.1 = ((bf16[256,4,512]{2,0,1:T(8,128)(2,1)}), bf16[256,4,512]{2,0,1:T(8,128)(2,1)}, u32[]{:S(2)}, u32[]{:S(2)}) async-start(bf16[256,4,512]{2,0,1:T(8,128)(2,1)} %bitcast.660), calls=%async_computation.1 | async-start | bytes 2097152 | tf_op jit(solution)/shard_map/all_to_all | solution.py:165
  56.3 56.5 %all-to-all-start.4 = ((bf16[256,4,512]{2,0,1:T(8,128)(2,1)}), bf16[256,4,512]{2,0,1:T(8,128)(2,1)}, u32[]{:S(2)}, u32[]{:S(2)}) async-start(bf16[256,4,512]{2,0,1:T(8,128)(2,1)} %bitcast.657), calls=%async_computation.4 | async-start | bytes 2097152 | tf_op jit(solution)/shard_map/all_to_all | solution.py:164
  78.0 20.0 %copy-start.54 = (f32[2,16,4,16,16]{4,3,2,1,0:T(8,128)}, f32[2,16,4,16,16]{4,3,2,1,0:T(8,128)S(1)}, u32[]{:S(2)}) copy-start(f32[2,16,4,16,16]{4,3,2,1,0:T(8,128)S(1)} %get-tuple-element.309) | copy-start | bytes 393220
  87.0 91.2 %copy-start.89 = (f32[16,1,3,16]{2,1,3,0:T(1,128)}, f32[16,1,3,16]{2,1,3,0:T(1,128)S(1)}, u32[]{:S(2)}) copy-start(f32[16,1,3,16]{2,1,3,0:T(1,128)S(1)} %slice.607) | copy-start | bytes 9220
  112.8 22.5 %all-to-all-start.5 = ((bf16[256,4,512]{2,0,1:T(8,128)(2,1)}), bf16[256,4,512]{2,0,1:T(8,128)(2,1)}, u32[]{:S(2)}, u32[]{:S(2)}) async-start(bf16[256,4,512]{2,0,1:T(8,128)(2,1)} %bitcast.736), calls=%async_computation.5 | async-start | bytes 2097152 | tf_op jit(solution)/shard_map/all_to_all | solution.py:166
  135.3 74.6 %all-to-all-start.3 = ((bf16[256,4,512]{2,0,1:T(8,128)(2,1)}), bf16[256,4,512]{2,0,1:T(8,128)(2,1)}, u32[]{:S(2)}, u32[]{:S(2)}) async-start(bf16[256,4,512]{2,0,1:T(8,128)(2,1)} %bitcast.658), calls=%async_computation.3 | async-start | bytes 2097152 | tf_op jit(solution)/shard_map/all_to_all | solution.py:169
  139.6 186.7 %all-gather.9.cloned.1.call-start = ((), (), s32[]{:S(2)}) async-start(), calls=%async_computation.12 | async-start | bytes 1179648 | tf_op jit(solution)/shard_map/all_gather | solution.py:19
  141.1 21.0 %copy-start.28 = (bf16[16,64,4,128]{3,2,1,0:T(4,128)(2,1)}, bf16[16,64,4,128]{3,2,1,0:T(4,128)(2,1)S(1)}, u32[]{:S(2)}) copy-start(bf16[16,64,4,128]{3,2,1,0:T(4,128)(2,1)S(1)} %reshape.1032) | copy-start | bytes 3145732
  176.9 149.4 %all-gather.13.cloned.1.call-start = ((), (), s32[]{:S(2)}) async-start(), calls=%async_computation.14 | async-start | bytes 1179648 | tf_op jit(solution)/shard_map/all_gather | solution.py:19
  249.2 86.3 %all-gather.7.cloned.1.call-start = ((), (), s32[]{:S(2)}) async-start(), calls=%async_computation.11 | async-start | bytes 1179648 | tf_op jit(solution)/shard_map/all_gather | solution.py:19
  267.2 106.7 %all-gather.11.cloned.1.call-start = ((), (), s32[]{:S(2)}) async-start(), calls=%async_computation.13 | async-start | bytes 1179648 | tf_op jit(solution)/shard_map/all_gather | solution.py:19
  533.1 31.9 %copy-start.25 = (f32[16,4,64,128]{3,2,1,0:T(8,128)}, f32[16,4,64,128]{3,2,1,0:T(8,128)S(1)}, u32[]{:S(2)}) copy-start(f32[16,4,64,128]{3,2,1,0:T(8,128)S(1)} %fusion.60) | copy-start | bytes 6291460
  546.6 18.4 %copy-start.21 = (f32[16,4,64,128]{3,2,1,0:T(8,128)}, f32[16,4,64,128]{3,2,1,0:T(8,128)S(1)}, u32[]{:S(2)}) copy-start(f32[16,4,64,128]{3,2,1,0:T(8,128)S(1)} %fusion.222) | copy-start | bytes 6291460
  576.4 30.7 %all-to-all-start.10 = ((bf16[4,256,4]{1,2,0:T(4,128)(2,1)}), bf16[4,256,4]{1,2,0:T(4,128)(2,1)S(1)}, u32[]{:S(2)}, u32[]{:S(2)}) async-start(bf16[4,256,4]{1,2,0:T(4,128)(2,1)} %copy.249), calls=%async_computation.10 | async-start | bytes 16384 | tf_op jit(solution)/shard_map/all_to_all | solution.py:275
  580.9 16.7 %copy-start.4 = (f32[16,64,4,128]{3,2,1,0:T(4,128)S(1)}, f32[16,64,4,128]{3,2,1,0:T(4,128)}, u32[]{:S(2)}) copy-start(f32[16,64,4,128]{3,2,1,0:T(4,128)} %reshape.1062) | copy-start | bytes 6291460
  581.0 16.7 %copy-start.14 = (f32[16,64,4,128]{3,2,1,0:T(4,128)S(1)}, f32[16,64,4,128]{3,2,1,0:T(4,128)}, u32[]{:S(2)}) copy-start(f32[16,64,4,128]{3,2,1,0:T(4,128)} %reshape.1063) | copy-start | bytes 6291460
  581.0 16.7 %copy-start.22 = (f32[16,4,64,128]{3,2,1,0:T(8,128)S(1)}, f32[16,4,64,128]{3,2,1,0:T(8,128)}, u32[]{:S(2)}) copy-start(f32[16,4,64,128]{3,2,1,0:T(8,128)} %copy-done.21) | copy-start | bytes 6291460
  607.1 18.0 %all-to-all-start.9 = ((bf16[4,256,512]{2,1,0:T(8,128)(2,1)}), bf16[4,256,512]{2,1,0:T(8,128)(2,1)S(1)}, u32[]{:S(2)}, u32[]{:S(2)}) async-start(bf16[4,256,512]{2,1,0:T(8,128)(2,1)} %convert_element_type.286), calls=%async_computation.9 | async-start | bytes 2097152 | tf_op jit(solution)/shard_map/all_to_all | solution.py:274
  625.1 18.8 %all-to-all-start.6 = ((bf16[4,256,512]{2,1,0:T(8,128)(2,1)}), bf16[4,256,512]{2,1,0:T(8,128)(2,1)}, u32[]{:S(2)}, u32[]{:S(2)}) async-start(bf16[4,256,512]{2,1,0:T(8,128)(2,1)} %convert_element_type.278), calls=%async_computation.6 | async-start | bytes 2097152 | tf_op jit(solution)/shard_map/all_to_all | solution.py:271
  643.9 18.0 %all-to-all-start.7 = ((bf16[4,256,512]{2,1,0:T(8,128)(2,1)}), bf16[4,256,512]{2,1,0:T(8,128)(2,1)S(1)}, u32[]{:S(2)}, u32[]{:S(2)}) async-start(bf16[4,256,512]{2,1,0:T(8,128)(2,1)} %convert_element_type.280), calls=%async_computation.7 | async-start | bytes 2097152 | tf_op jit(solution)/shard_map/all_to_all | solution.py:272
  648.5 17.5 %copy-start.85 = (bf16[4,256,512]{2,1,0:T(8,128)(2,1)S(1)}, bf16[4,256,512]{2,1,0:T(8,128)(2,1)}, u32[]{:S(2)}) copy-start(bf16[4,256,512]{2,1,0:T(8,128)(2,1)} %copy-done.84) | copy-start | bytes 3145732
  661.8 18.0 %all-to-all-start.8 = ((bf16[4,256,512]{2,1,0:T(8,128)(2,1)}), bf16[4,256,512]{2,1,0:T(8,128)(2,1)S(1)}, u32[]{:S(2)}, u32[]{:S(2)}) async-start(bf16[4,256,512]{2,1,0:T(8,128)(2,1)} %convert_element_type.283), calls=%async_computation.8 | async-start | bytes 2097152 | tf_op jit(solution)/shard_map/all_to_all | solution.py:273
  (153 other events, 680.5 us)
Sparse Core Ops, SparseCore 0:
  177.0 42.4 all-gather.8
  249.4 42.4 all-gather.12
  294.0 38.8 all-gather.6
  334.9 38.8 all-gather.10
where the time goes:
time: 701 us; the launch traced here: 689 us
  matrix products  249 us (36%)
  local copies, waits for them, and re-layouts  180 us (26%)
  waiting for transfers between devices  98.9 us (14%)
  other arithmetic  98.2 us (14%)
  starting transfers between devices  43.4 us (6%)
  between operations  16.9 us (2%)
    dot_general x89, matrix products, matrix_product(): return jnp.einsum(form, left, right, precision=PRECISE)  249 us
    another operation x12, local copies, waits for them, and re-layouts, substitute(): earlier_rows = jnp.stack(found_rows)  50.1 us
    all_gather x4, waiting for transfers between devices, entering(): lax.all_gather(a.astype(kind), axis)  38.3 us
    reduce_sum x15, other arithmetic, substitute(): flattened[row_index, :row_index][:, None, :] * earlier_rows  27.2 us
    reduce_sum x28, other arithmetic, substitute(): jnp.sum(flattened[row_index, :row_index][:, None, :] * earlier_rows, axis=0)  24.5 us
    unnamed x332, local copies, waits for them, and re-layouts  21.9 us
    slice x16, local copies, waits for them, and re-layouts, substitute(): flattened[row_index, :row_index][:, None, :] * earlier_rows  19.8 us
  transfers between devices with their start and end apart: 15, of which 7 were waited for; matrix products, arithmetic and copies ran while one was open for 46% of the time, Pallas kernels for 0%

commit v1 on v0

v1 whole, which is shorter than its diff:
```python
import functools

import jax
import jax.numpy as jnp
from jax import lax
from jax.experimental import pallas as pl
from jax.experimental.pallas import tpu as pltpu
from jax.sharding import PartitionSpec as P

DK = 128
DV = 128
SPAN = 128
ROWS = 3 * DK + 16
F32 = jnp.float32
BF16 = jnp.bfloat16


def split(x):
    if isinstance(x, tuple):
        return x
    if x.dtype == BF16:
        return (x, None)
    high = x.astype(BF16)
    return (high, (x - high.astype(F32)).astype(BF16))


def product(left, right, left_dim, right_dim):
    left_high, left_low = split(left)
    right_high, right_low = split(right)
    lefts, rights = [left_high], [right_high]
    if left_low is not None:
        lefts.append(left_low)
        rights.append(right_high)
    if right_low is not None:
        lefts.append(left_high)
        rights.append(right_low)
    if len(lefts) > 1:
        left_all = jnp.concatenate(lefts, axis=left_dim)
        right_all = jnp.concatenate(rights, axis=right_dim)
    else:
        left_all, right_all = left_high, right_high
    return lax.dot_general(
        left_all, right_all, (((left_dim,), (right_dim,)), ((), ())), preferred_element_type=F32
    )


def nn(left, right):
    return product(left, right, 1, 0)


def nt(left, right):
    return product(left, right, 1, 1)


def tn(left, right):
    return product(left, right, 0, 0)


def iotas(n=SPAN):
    return (
        lax.broadcasted_iota(jnp.int32, (n, n), 0),
        lax.broadcasted_iota(jnp.int32, (n, n), 1),
    )


def diagonal(row):
    rows, cols = iotas()
    return jnp.where(rows == cols, row, 0.0)


def column(row):
    return jnp.sum(diagonal(row), axis=1, keepdims=True)


def unit_lower_inverses(strict):
    rows, cols = iotas()
    unit = jnp.where(rows == cols, 1.0, 0.0)
    found = None
    size = 1
    while size < SPAN:
        inside = (
            (rows // (2 * size) == cols // (2 * size))
            & ((rows // size) % 2 == 1)
            & ((cols // size) % 2 == 0)
        )
        corners = [jnp.where(inside, n, 0.0) for n in strict]
        if found is None:
            found = [unit - c for c in corners]
        else:
            parts = [split(x) for x in found]
            inner = [nn(c, x) for c, x in zip(corners, parts)]
            found = [x - nn(p, i) for x, p, i in zip(found, parts, inner)]
        size *= 2
    return found


def span_tables(q, k, g, beta):
    rows, cols = iotas()
    lower = jnp.where(rows >= cols, 1.0, 0.0).astype(BF16)
    running = nn(lower, g)
    middle = running[SPAN // 2 : SPAN // 2 + 1, :]
    ending = running[SPAN - 1 : SPAN, :]
    up = jnp.exp(running - middle)
    down = jnp.exp(middle - running)
    start_factor = jnp.exp(middle)
    end_factor = jnp.exp(ending - middle)
    k = k.astype(F32)
    key_up = k * up
    query_up = q.astype(F32) * up
    key_down = k * down
    key_write = key_down * beta
    return dict(
        up=up,
        down=down,
        start_factor=start_factor,
        end_factor=end_factor,
        final=jnp.exp(ending),
        key_up=key_up,
        query_up=query_up,
        key_down=key_down,
        key_write=key_write,
        key_offset=key_up * start_factor,
        query_offset=query_up * start_factor,
        key_end=key_write * end_factor,
    )


def head_betas(beta_ref, head):
    heads = beta_ref.shape[1]
    picked = jnp.where(
        lax.broadcasted_iota(jnp.int32, (heads, DK), 0) == head, 1.0, 0.0
    ).astype(BF16)
    return nn(beta_ref[...], picked)


def block_kernel(batch, me_ref, q_ref, k_ref, v_ref, g_ref, do_ref, beta_ref, msg_ref, ux_ref, ar_ref):
    del me_ref
    step = pl.program_id(0)
    spans = q_ref.shape[0] // SPAN
    rows, cols = iotas()
    places = [(h, n) for h in range(batch) for n in range(spans)]
    betas = [head_betas(beta_ref, step * batch + h) for h in range(batch)]
    tables, strict, reach = {}, {}, {}
    for h, n in places:
        at = (slice(n * SPAN, (n + 1) * SPAN), slice(h * DK, (h + 1) * DK))
        t = span_tables(q_ref[at], k_ref[at], g_ref[at], betas[h][at[0]])
        both = nt(jnp.concatenate([t["key_up"], t["query_up"]], axis=0), t["key_write"])
        strict[h, n] = jnp.where(rows > cols, both[:SPAN], 0.0)
        reach[h, n] = jnp.where(rows >= cols, both[SPAN:], 0.0)
        tables[h, n] = t
    inverses = dict(zip(places, unit_lower_inverses([strict[p] for p in places])))
    solved = {}
    for h, n in places:
        at = (slice(n * SPAN, (n + 1) * SPAN), slice(h * DK, (h + 1) * DK))
        ar_ref[at[0], h * 2 * SPAN : h * 2 * SPAN + SPAN] = inverses[h, n]
        ar_ref[at[0], h * 2 * SPAN + SPAN : (h + 1) * 2 * SPAN] = reach[h, n]
        inverse = split(inverses[h, n])
        solved[h, n] = (nn(inverse, tables[h, n]["key_offset"]), nn(inverse, v_ref[at]))
    state, read = {}, {}
    for n in range(spans):
        for h in range(batch):
            t = tables[h, n]
            across, own = solved[h, n]
            reach_parts = split(reach[h, n])
            at = slice(n * SPAN, (n + 1) * SPAN)
            if n == 0:
                ux = jnp.concatenate([-across, own], axis=1)
                out_map = t["query_offset"] + nn(reach_parts, ux[:, :DK])
                kept = jnp.concatenate([diagonal(t["final"]), jnp.zeros((DK, DV), F32)], axis=1)
            else:
                parts = split(state[h])
                moved = nn(across, parts)
                ux = jnp.concatenate([-moved[:, :DK], own - moved[:, DK:]], axis=1)
                out_map = nn(t["query_offset"], (parts[0][:, :DK], parts[1][:, :DK])) + nn(
                    reach_parts, ux[:, :DK]
                )
                kept = column(t["final"]) * state[h]
            ux_ref[at, h * 2 * DK : (h + 1) * 2 * DK] = ux
            state[h] = kept + tn(t["key_end"], ux)
            term = tn(out_map, do_ref[at, h * DV : (h + 1) * DV])
            read[h] = term if n == 0 else read[h] + term
    for h in range(batch):
        store_message(msg_ref, h, state[h][:, :DK], state[h][:, DK:], read[h])


def store_message(msg_ref, h, block_map, shift, read):
    rows, cols = iotas()
    rounded = block_map.astype(BF16)
    left = jnp.where(rows == cols, block_map - rounded.astype(F32), 0.0)
    msg_ref[h, 0:DK, :] = rounded
    msg_ref[h, DK : 2 * DK, :] = shift.astype(BF16)
    msg_ref[h, 2 * DK : 3 * DK, :] = read.astype(BF16)
    msg_ref[h, 3 * DK :, :] = jnp.broadcast_to(
        jnp.sum(left, axis=0, keepdims=True), (16, DK)
    ).astype(BF16)


def load_map(ref, *at):
    rows, cols = iotas()
    row = ref[at + (slice(3 * DK, ROWS), slice(None))][0:1, :].astype(F32)
    return (
        ref[at + (slice(0, DK), slice(None))],
        jnp.where(rows == cols, row, 0.0).astype(BF16),
    )


def load_shift(ref, *at):
    return ref[at + (slice(DK, 2 * DK), slice(None))]


def load_read(ref, *at):
    return ref[at + (slice(2 * DK, 3 * DK), slice(None))]


def whole_map(parts):
    return parts[0].astype(F32) + parts[1].astype(F32)


def backward_kernel(batch, q_ref, k_ref, g_ref, do_ref, beta_ref, ar_ref, wx_ref):
    step = pl.program_id(0)
    spans = q_ref.shape[0] // SPAN
    betas = [head_betas(beta_ref, step * batch + h) for h in range(batch)]
    carried = {}
    for n in range(spans - 1, -1, -1):
        for h in range(batch):
            at = (slice(n * SPAN, (n + 1) * SPAN), slice(h * DK, (h + 1) * DK))
            t = span_tables(q_ref[at], k_ref[at], g_ref[at], betas[h][at[0]])
            do = do_ref[at]
            inverse = split(ar_ref[at[0], h * 2 * SPAN : h * 2 * SPAN + SPAN])
            reach = ar_ref[at[0], h * 2 * SPAN + SPAN : (h + 1) * 2 * SPAN]
            own = tn(inverse, tn(reach, do))
            through = tn(inverse, t["key_end"])
            if n == spans - 1:
                wx = jnp.concatenate([through, own], axis=1)
            else:
                moved = nn(through, carried[h])
                wx = jnp.concatenate([moved[:, :DK], moved[:, DK:] + own], axis=1)
            wx_ref[at[0], h * 2 * DK : (h + 1) * 2 * DK] = wx
            if n > 0:
                read = tn(t["query_offset"], do)
                if n == spans - 1:
                    kept = jnp.concatenate([diagonal(t["final"]), read], axis=1)
                else:
                    kept = column(t["final"]) * carried[h]
                    kept = jnp.concatenate([kept[:, :DK], kept[:, DK:] + read], axis=1)
                carried[h] = kept - tn(t["key_offset"], wx)


def compose_kernel(me_ref, parts_ref, total_ref):
    me = me_ref[0]
    count, heads = parts_ref.shape[:2]
    for h in range(heads):
        first = load_map(parts_ref, me, h)
        state = jnp.concatenate([whole_map(first), load_shift(parts_ref, me, h).astype(F32)], axis=1)
        for j in range(1, count):
            at = jnp.bitwise_xor(me, j)
            moved = nn(load_map(parts_ref, at, h), state)
            state = jnp.concatenate(
                [moved[:, :DK], moved[:, DK:] + load_shift(parts_ref, at, h).astype(F32)], axis=1
            )
        read = load_read(parts_ref, jnp.bitwise_xor(me, count - 1), h).astype(F32)
        for j in range(count - 2, -1, -1):
            at = jnp.bitwise_xor(me, j)
            read = tn(load_map(parts_ref, at, h), read) + load_read(parts_ref, at, h).astype(F32)
        store_message(total_ref, h, state[:, :DK], state[:, DK:], read)


def join_kernel(first, last, upper_ref, own_ref, other_ref, carry_ref, total_ref, next_ref):
    heads = own_ref.shape[0]
    rows, cols = iotas()
    unit = jnp.where(rows == cols, 1.0, 0.0)

    def part(i):
        return slice(i * DK, (i + 1) * DK)

    @pl.when(upper_ref[0] == 1)
    def _():
        for h in range(heads):
            early = load_map(other_ref, h)
            shift = load_shift(other_ref, h)
            if first:
                next_ref[h, part(1)] = shift.astype(F32)
                next_ref[h, part(2)] = jnp.zeros((DK, DV), F32)
                next_ref[h, part(0)] = whole_map(early)
                next_ref[h, part(3)] = unit
            else:
                before = carry_ref[h, part(0)]
                next_ref[h, part(1)] = nn(before, shift) + carry_ref[h, part(1)]
                next_ref[h, part(2)] = carry_ref[h, part(2)]
                if not last:
                    next_ref[h, part(0)] = nn(before, early)
                    next_ref[h, part(3)] = carry_ref[h, part(3)]
            if not last:
                late = load_map(own_ref, h)
                store_message(
                    total_ref,
                    h,
                    nn(late, early),
                    nn(late, shift) + load_shift(own_ref, h).astype(F32),
                    load_read(other_ref, h).astype(F32) + tn(early, load_read(own_ref, h)),
                )

    @pl.when(upper_ref[0] == 0)
    def _():
        for h in range(heads):
            late = load_map(other_ref, h)
            read = load_read(other_ref, h)
            if first:
                next_ref[h, part(1)] = jnp.zeros((DK, DV), F32)
                next_ref[h, part(2)] = read.astype(F32)
                next_ref[h, part(0)] = unit
                next_ref[h, part(3)] = whole_map(late)
            else:
                after = carry_ref[h, part(3)]
                next_ref[h, part(2)] = tn(after, read) + carry_ref[h, part(2)]
                next_ref[h, part(1)] = carry_ref[h, part(1)]
                if not last:
                    next_ref[h, part(3)] = nn(late, after)
                    next_ref[h, part(0)] = carry_ref[h, part(0)]
            if not last:
                early = load_map(own_ref, h)
                store_message(
                    total_ref,
                    h,
                    nn(late, early),
                    nn(late, load_shift(own_ref, h)) + load_shift(other_ref, h).astype(F32),
                    load_read(own_ref, h).astype(F32) + tn(early, read),
                )


def spread_kernel(me_ref, parts_ref, carry_ref, out_ref):
    me = me_ref[0]
    count, heads = parts_ref.shape[:2]
    for h in range(heads):
        state = carry_ref[h, DK : 2 * DK]
        for j in range(count):
            at = jnp.bitwise_xor(me, j)
            out_ref[at, h, 0:DK] = state.astype(BF16)
            if j < count - 1:
                state = nn(load_map(parts_ref, at, h), state) + load_shift(parts_ref, at, h).astype(F32)
        grad = carry_ref[h, 2 * DK : 3 * DK]
        for j in range(count - 1, -1, -1):
            at = jnp.bitwise_xor(me, j)
            out_ref[at, h, DK:] = grad.astype(BF16)
            if j > 0:
                grad = tn(load_map(parts_ref, at, h), grad) + load_read(parts_ref, at, h).astype(F32)


def gradient_kernel(
    batch, me_ref, q_ref, k_ref, g_ref, do_ref, beta_ref, ux_ref, wx_ref, ends_ref,
    dq_ref, dk_ref, dv_ref, dg_ref, db_ref,
):
    del me_ref
    step = pl.program_id(0)
    tokens = q_ref.shape[0]
    spans = tokens // SPAN
    rows, cols = iotas()
    upper = jnp.where(rows <= cols, 1.0, 0.0).astype(BF16)
    ones = jnp.ones((8, DV), BF16)
    lanes = lax.broadcasted_iota(jnp.int32, (tokens, beta_ref.shape[1]), 1)

    @pl.when(step == 0)
    def _():
        db_ref[...] = jnp.zeros_like(db_ref)

    all_gates = db_ref[...]
    for h in range(batch):
        head = step * batch + h
        beta = head_betas(beta_ref, head)
        wide = slice(h * DK, (h + 1) * DK)
        start = ends_ref[0, h, 0:DK]
        end = ends_ref[0, h, DK:]
        ux = ux_ref[:, h * 2 * DK : (h + 1) * 2 * DK]
        wx = wx_ref[:, h * 2 * DK : (h + 1) * 2 * DK]
        written = ux[:, DK:] + nn(ux[:, :DK], start)
        grad_write = wx[:, DK:] + nn(wx[:, :DK], end)
        dv_ref[:, wide] = grad_write.astype(BF16)
        tables, us, lefts = [], [], []
        for n in range(spans):
            at = slice(n * SPAN, (n + 1) * SPAN)
            tables.append(span_tables(q_ref[at, wide], k_ref[at, wide], g_ref[at, wide], beta[at]))
            us.append(split(written[at]))
            high, low = split(-grad_write[at])
            do = do_ref[at, wide]
            lefts.append((high, low, do))
        states, grads = [start], [None] * spans
        state = start.astype(F32)
        for n in range(spans - 1):
            state = column(tables[n]["final"]) * state + tn(tables[n]["key_end"], us[n])
            states.append(split(state))
        grads[spans - 1] = end
        grad = end.astype(F32)
        for n in range(spans - 1, 0, -1):
            high, low, do = lefts[n]
            grad = (
                column(tables[n]["final"]) * grad
                + tn(tables[n]["query_offset"], do)
                + tn(tables[n]["key_offset"], (high, low))
            )
            grads[n - 1] = split(grad)
        gates = []
        for n in range(spans):
            at = slice(n * SPAN, (n + 1) * SPAN)
            t = tables[n]
            high, low, do = lefts[n]
            left = (
                jnp.concatenate([high, do], axis=0),
                jnp.concatenate([low, jnp.zeros_like(low)], axis=0),
            )
            from_state = nt(left, states[n])
            pairs = nt(left, us[n])
            grad_end = nt(us[n], grads[n])
            pairs = jnp.concatenate(
                [jnp.where(rows > cols, pairs[:SPAN], 0.0), jnp.where(rows >= cols, pairs[SPAN:], 0.0)],
                axis=0,
            )
            pairs = split(pairs)
            ups = nn(pairs, t["key_write"])
            key_up_grad = ups[:SPAN] + from_state[:SPAN] * t["start_factor"]
            query_up_grad = ups[SPAN:] + from_state[SPAN:] * t["start_factor"]
            write_grad = (
                tn(pairs, jnp.concatenate([t["key_up"], t["query_up"]], axis=0))
                + grad_end * t["end_factor"]
            )
            dq_ref[at, wide] = (query_up_grad * t["up"]).astype(BF16)
            dk_ref[at, wide] = (key_up_grad * t["up"] + write_grad * t["down"] * beta[at]).astype(BF16)
            gates.append(jnp.sum(write_grad * t["key_down"], axis=1, keepdims=True))
            flow = query_up_grad * t["query_up"] + key_up_grad * t["key_up"] - write_grad * t["key_write"]
            span_state = whole(states[n])
            span_grad = whole(grads[n])
            last = jnp.sum(grad_end * t["key_end"], axis=0, keepdims=True) + t["final"] * nt(
                ones, span_state * span_grad
            )[0:1]
            dg_ref[at, wide] = (nn(upper, flow) + last).astype(BF16)
        gate = jnp.concatenate(gates, axis=0)
        all_gates = jnp.where(lanes == head, gate, all_gates.astype(F32)).astype(BF16)
    db_ref[...] = all_gates


def whole(x):
    if isinstance(x, tuple):
        return x[0].astype(F32) + x[1].astype(F32)
    return x.astype(F32)


def params(semantics=("arbitrary",)):
    return pltpu.CompilerParams(dimension_semantics=semantics, vmem_limit_bytes=56 << 20)


def cost(flops, data):
    return pl.CostEstimate(flops=int(flops), bytes_accessed=int(data), transcendentals=0)


def local(queries, key_rows, value_matrix, log_decay, beta_gate, grad_out):
    tokens, heads = beta_gate.shape
    count = lax.axis_size("head")
    blocks = lax.axis_size("seq")
    mine = heads // count
    batch = 2 if mine % 2 == 0 else 1
    per = mine // batch
    steps = heads // batch
    me = lax.axis_index("head").astype(jnp.int32)
    place = lax.axis_index("seq").astype(jnp.int32)
    me_row = me.reshape(1)
    flops = 2 * 3 * steps * batch * tokens * DK * DK

    def wide(columns):
        return pl.BlockSpec((tokens, batch * columns), lambda i, *_: (0, i))

    beta_spec = pl.BlockSpec((tokens, heads), lambda i, *_: (0, 0))

    def ordered(rows):
        return pl.BlockSpec(
            (None, batch, rows, DK),
            lambda i, m: (jnp.bitwise_xor(i // per, m[0]), i % per, 0, 0),
        )

    messages, ux, ar = pl.pallas_call(
        functools.partial(block_kernel, batch),
        grid_spec=pltpu.PrefetchScalarGridSpec(
            num_scalar_prefetch=1,
            grid=(steps,),
            in_specs=[wide(DK), wide(DK), wide(DV), wide(DK), wide(DV), beta_spec],
            out_specs=[ordered(ROWS), wide(2 * DK), wide(2 * SPAN)],
        ),
        out_shape=[
            jax.ShapeDtypeStruct((count, mine, ROWS, DK), BF16),
            jax.ShapeDtypeStruct((tokens, heads * 2 * DK), F32),
            jax.ShapeDtypeStruct((tokens, heads * 2 * SPAN), F32),
        ],
        compiler_params=params(),
        cost_estimate=cost(24 * flops, 20 << 20),
        name="block_maps",
    )(me_row, queries, key_rows, value_matrix, log_decay, grad_out, beta_gate)

    def exchange(parts):
        return jnp.stack(
            [parts[0]]
            + [
                lax.ppermute(parts[d], "head", [(i, i ^ d) for i in range(count)])
                for d in range(1, count)
            ]
        )

    gathered = exchange(messages)

    wx = pl.pallas_call(
        functools.partial(backward_kernel, batch),
        grid_spec=pltpu.PrefetchScalarGridSpec(
            num_scalar_prefetch=0,
            grid=(steps,),
            in_specs=[wide(DK), wide(DK), wide(DK), wide(DV), beta_spec, wide(2 * SPAN)],
            out_specs=wide(2 * DK),
        ),
        out_shape=jax.ShapeDtypeStruct((tokens, heads * 2 * DK), F32),
        compiler_params=params(),
        cost_estimate=cost(8 * flops, 12 << 20),
        name="backward_maps",
    )(queries, key_rows, log_decay, grad_out, beta_gate, ar)

    smem = pl.BlockSpec(memory_space=pltpu.SMEM)
    vmem = pl.BlockSpec(memory_space=pltpu.VMEM)
    total_shape = jax.ShapeDtypeStruct((mine, ROWS, DK), BF16)
    carry_shape = jax.ShapeDtypeStruct((mine, 4 * DK, DK), F32)
    total = pl.pallas_call(
        compose_kernel,
        in_specs=[smem, vmem],
        out_specs=vmem,
        out_shape=total_shape,
        compiler_params=pltpu.CompilerParams(vmem_limit_bytes=40 << 20),
        name="compose",
    )(me_row, gathered)
    carry = jnp.zeros(carry_shape.shape, F32)
    distance = 1
    while distance < blocks:
        first, last = distance == 1, 2 * distance >= blocks
        other = lax.ppermute(total, "seq", [(i, i ^ distance) for i in range(blocks)])
        upper = (jnp.bitwise_and(place, distance) != 0).astype(jnp.int32).reshape(1)
        total, carry = pl.pallas_call(
            functools.partial(join_kernel, first, last),
            in_specs=[smem, vmem, vmem, vmem],
            out_specs=[vmem, vmem],
            out_shape=[total_shape, carry_shape],
            compiler_params=pltpu.CompilerParams(vmem_limit_bytes=40 << 20),
            name="join",
        )(upper, total, other, carry)
        distance *= 2
    ends = pl.pallas_call(
        spread_kernel,
        in_specs=[smem, vmem, vmem],
        out_specs=vmem,
        out_shape=jax.ShapeDtypeStruct((count, mine, 2 * DK, DV), BF16),
        compiler_params=pltpu.CompilerParams(vmem_limit_bytes=40 << 20),
        name="spread",
    )(me_row, gathered, carry)
    ends = exchange(ends)

    token_shape = jax.ShapeDtypeStruct(queries.shape, BF16)
    return pl.pallas_call(
        functools.partial(gradient_kernel, batch),
        grid_spec=pltpu.PrefetchScalarGridSpec(
            num_scalar_prefetch=1,
            grid=(steps,),
            in_specs=[
                wide(DK), wide(DK), wide(DK), wide(DV), beta_spec, wide(2 * DK), wide(2 * DK),
                pl.BlockSpec(
                    (1, batch, 2 * DK, DV),
                    lambda i, m: (jnp.bitwise_xor(i // per, m[0]), i % per, 0, 0),
                ),
            ],
            out_specs=[wide(DK), wide(DK), wide(DV), wide(DK), beta_spec],
        ),
        out_shape=[
            token_shape, token_shape, token_shape, token_shape,
            jax.ShapeDtypeStruct(beta_gate.shape, BF16),
        ],
        compiler_params=params(),
        cost_estimate=cost(16 * flops, 20 << 20),
        name="gradients",
    )(me_row, queries, key_rows, log_decay, grad_out, beta_gate, ux, wx, ends)


def solution(mesh):
    spec = P(("seq", "head"), None)
    return jax.shard_map(
        lambda *arrays: tuple(local(*arrays)),
        mesh=mesh,
        in_specs=(spec,) * 6,
        out_specs=(spec,) * 5,
        check_vma=False,
    )
```

time: 701 us -> 163 us (0.23); the launches traced: 689 us -> 163 us
  matrix products: 249 us -> 0 us
  local copies, waits for them, and re-layouts: 180 us -> 8.5 us
  other arithmetic: 98.2 us -> 1.4 us
  Pallas kernels: 0 us -> 86.5 us
  waiting for transfers between devices: 98.9 us -> 54 us
  starting transfers between devices: 43.4 us -> 11.8 us
  between operations: 16.9 us -> 0.72 us
    dot_general x89 -> x0, matrix products: 249 us -> none  [matrix_product(): return jnp.einsum(form, left, right, precision=PRECISE)]
    pallas_call x0 -> x8, Pallas kernels: none -> 86.5 us  [the longest x1 38.4 us: local(): pl.pallas_call(functools.partial(block_kernel, batch), grid_spec=pltpu.Pr...]
    all_to_all x11 -> x0, waiting for transfers between devices: 60.5 us -> none  [the longest x1 12.1 us: local(): lax.all_to_all(restore(grad_key), 'head', split_axis=0, concat_axis=1, ti...]
    another operation x18 -> x0, local copies, waits for them, and re-layouts: 59.9 us -> none  [the longest x12 50.1 us: substitute(): earlier_rows = jnp.stack(found_rows)]
    ppermute x0 -> x9, waiting for transfers between devices: none -> 54 us  [the longest x3 35.9 us: local(): lax.ppermute(total, 'seq', [(i, i ^ distance) for i in range(blocks)])]
    reduce_sum x45 -> x0, other arithmetic: 53.5 us -> none  [the longest x15 27.2 us: substitute(): flattened[row_index, :row_index][:, None, :] * earlier_rows]
    all_to_all x11 -> x0, starting transfers between devices: 43 us -> none  [the longest x1 4.27 us: local(): lax.all_to_all(grad_out, 'head', split_axis=1, concat_axis=0, tiled=True)]
    all_gather x4 -> x0, waiting for transfers between devices: 38.3 us -> none  [entering(): lax.all_gather(a.astype(kind), axis)]
  transfers between devices with their start and end apart: 15 -> 9, of which waited for: 7 -> 5; matrix products, arithmetic and copies ran while one was open for 46% -> 0% of each run, Pallas kernels for 0% -> 8%
where the time goes in v1:
time: 163 us
  Pallas kernels  86.5 us (53%)
  waiting for transfers between devices  54 us (33%)
  starting transfers between devices  11.8 us (7%)
  local copies, waits for them, and re-layouts  8.5 us (5%)
    pallas_call x1, Pallas kernels, local(): pl.pallas_call(functools.partial(block_kernel, batch), grid_spec=pltpu.Pr...  38.4 us
    ppermute x3, waiting for transfers between devices, local(): lax.ppermute(total, 'seq', [(i, i ^ distance) for i in range(blocks)])  35.9 us
    pallas_call x1, Pallas kernels, local(): pl.pallas_call(functools.partial(gradient_kernel, batch), grid_spec=pltpu...  26.6 us
    ppermute x6, waiting for transfers between devices, exchange(): lax.ppermute(parts[d], 'head', [(i, i ^ d) for i in range(count)])  18.1 us
    pallas_call x1, Pallas kernels, local(): pl.pallas_call(functools.partial(backward_kernel, batch), grid_spec=pltpu...  13.5 us
    ppermute x3, starting transfers between devices, local(): lax.ppermute(total, 'seq', [(i, i ^ distance) for i in range(blocks)])  6.72 us
    unnamed x9, local copies, waits for them, and re-layouts  5.36 us
    ppermute x6, starting transfers between devices, exchange(): lax.ppermute(parts[d], 'head', [(i, i ^ d) for i in range(count)])  5.08 us
  transfers between devices with their start and end apart: 9, of which 5 were waited for; matrix products, arithmetic and copies ran while one was open for 0% of the time, Pallas kernels for 8%

profile of v1, /device:TPU:0, one launch (start us, length us, event | category | flops | bytes accessed | tf_op | source)
XLA Modules:
  0.0 162.9 jit_solution(3907541700713174075)
XLA Ops:
  0.6 1.4 copy.13.beta_ref
  2.1 38.4 %block_maps.1 = (bf16[4,4,400,128]{3,2,1,0:T(8,128)(2,1)}, f32[256,4096]{1,0:T(8,128)}, f32[256,4096]{1,0:T(8,128)}) custom-call(s32[1]{0:T(128)} %bitcast.me_ref, bf16[256,2048]{1,0:T(8,128)(2,1)} %q_ref.5, bf16[256,2048]{1,0:T(8,128)(2,1)} %k_ref.5, bf16[256,2048]{1,0:T(8,128)(2,1)} %v_ref.1, bf16[256,2048]{1,0:T(8,128)(2,1)} %g_ref.5, ...), custom_call_target="tpu_custom_call" | custom-call | flops 9663676416 | bytes 20971520 | tf_op jit(solution)/shard_map/block_maps/pallas_call | solution.py:478
  40.5 1.5 fusion
  42.0 2.4 %collective-permute-start.2 = (bf16[4,400,128]{2,1,0:T(8,128)(2,1)S(1)}, bf16[4,400,128]{2,1,0:T(8,128)(2,1)S(1)}, u32[]{:S(2)}, u32[]{:S(2)}) collective-permute-start(bf16[4,400,128]{2,1,0:T(8,128)(2,1)S(1)} %get-tuple-element.27), channel_id=1, source_target_pairs={{0,3},{1,2},{2,1},{3,0},{4,7},{5,6},{6,5},{7,4},{8,11},{9,10},{10,... | collective-permute-start | bytes 1228808 | tf_op jit(solution)/shard_map/ppermute | solution.py:500
  45.1 9.1 %collective-permute-done.2 = bf16[4,400,128]{2,1,0:T(8,128)(2,1)S(1)} collective-permute-done((bf16[4,400,128]{2,1,0:T(8,128)(2,1)S(1)}, bf16[4,400,128]{2,1,0:T(8,128)(2,1)S(1)}, u32[]{:S(2)}, u32[]{:S(2)}) %collective-permute-start.2) | collective-permute-done | bytes 409632 | tf_op jit(solution)/shard_map/ppermute | solution.py:500
  54.3 9.0 %collective-permute-done.1 = bf16[4,400,128]{2,1,0:T(8,128)(2,1)S(1)} collective-permute-done((bf16[4,400,128]{2,1,0:T(8,128)(2,1)S(1)}, bf16[4,400,128]{2,1,0:T(8,128)(2,1)S(1)}, u32[]{:S(2)}, u32[]{:S(2)}) %collective-permute-start.1) | collective-permute-done | bytes 409632 | tf_op jit(solution)/shard_map/ppermute | solution.py:500
  63.4 2.8 %compose.1.own_ref = bf16[4,400,128]{2,1,0:T(8,128)(2,1)S(1)} custom-call(s32[1]{0:T(128)} %bitcast.me_ref, bf16[4,4,400,128]{3,2,1,0:T(8,128)(2,1)S(1)} %pad_maximum_fusion.parts_ref), custom_call_target="tpu_custom_call" | custom-call | tf_op jit(solution)/shard_map/compose/pallas_call | solution.py:525
  66.2 2.4 %collective-permute-start.3 = (bf16[4,400,128]{2,1,0:T(8,128)(2,1)S(1)}, bf16[4,400,128]{2,1,0:T(8,128)(2,1)S(1)}, u32[]{:S(2)}, u32[]{:S(2)}) collective-permute-start(bf16[4,400,128]{2,1,0:T(8,128)(2,1)S(1)} %compose.1.own_ref), channel_id=1, source_target_pairs={{0,4},{4,0},{8,12},{12,8},{16,20},{20,16},{24,28},{28,24},{1,5},{5... | collective-permute-start | bytes 1228808 | tf_op jit(solution)/shard_map/ppermute | solution.py:537
  68.6 9.7 %collective-permute-done.3.other_ref = bf16[4,400,128]{2,1,0:T(8,128)(2,1)S(1)} collective-permute-done((bf16[4,400,128]{2,1,0:T(8,128)(2,1)S(1)}, bf16[4,400,128]{2,1,0:T(8,128)(2,1)S(1)}, u32[]{:S(2)}, u32[]{:S(2)}) %collective-permute-start.3) | collective-permute-done | bytes 409632 | tf_op jit(solution)/shard_map/ppermute | solution.py:537
  78.8 1.0 copy-done
  79.8 1.8 %collective-permute-start.4 = (bf16[4,400,128]{2,1,0:T(8,128)(2,1)S(1)}, bf16[4,400,128]{2,1,0:T(8,128)(2,1)S(1)}, u32[]{:S(2)}, u32[]{:S(2)}) collective-permute-start(bf16[4,400,128]{2,1,0:T(8,128)(2,1)S(1)} %get-tuple-element.16.own_ref), channel_id=1, source_target_pairs={{0,8},{4,12},{8,0},{12,4},{16,24},{20,28},{24,16},{28,20},{1,9},{5... | collective-permute-start | bytes 1228808 | tf_op jit(solution)/shard_map/ppermute | solution.py:537
  81.6 9.1 %collective-permute-done.4.other_ref = bf16[4,400,128]{2,1,0:T(8,128)(2,1)S(1)} collective-permute-done((bf16[4,400,128]{2,1,0:T(8,128)(2,1)S(1)}, bf16[4,400,128]{2,1,0:T(8,128)(2,1)S(1)}, u32[]{:S(2)}, u32[]{:S(2)}) %collective-permute-start.4) | collective-permute-done | bytes 409632 | tf_op jit(solution)/shard_map/ppermute | solution.py:537
  90.7 0.7 copy-done.2
  91.4 1.2 copy-done.1
  92.6 1.0 copy-done.3
  94.2 2.5 %collective-permute-start.5 = (bf16[4,400,128]{2,1,0:T(8,128)(2,1)S(1)}, bf16[4,400,128]{2,1,0:T(8,128)(2,1)S(1)}, u32[]{:S(2)}, u32[]{:S(2)}) collective-permute-start(bf16[4,400,128]{2,1,0:T(8,128)(2,1)S(1)} %get-tuple-element.18.own_ref), channel_id=1, source_target_pairs={{0,16},{4,20},{8,24},{12,28},{16,0},{20,4},{24,8},{28,12},{1,17},{... | collective-permute-start | bytes 1228808 | tf_op jit(solution)/shard_map/ppermute | solution.py:537
  96.8 17.2 %collective-permute-done.5.other_ref = bf16[4,400,128]{2,1,0:T(8,128)(2,1)S(1)} collective-permute-done((bf16[4,400,128]{2,1,0:T(8,128)(2,1)S(1)}, bf16[4,400,128]{2,1,0:T(8,128)(2,1)S(1)}, u32[]{:S(2)}, u32[]{:S(2)}) %collective-permute-start.5) | collective-permute-done | bytes 409632 | tf_op jit(solution)/shard_map/ppermute | solution.py:537
  113.9 1.2 join.5
  115.1 2.9 %spread.1 = bf16[4,4,256,128]{3,2,1,0:T(8,128)(2,1)S(1)} custom-call(s32[1]{0:T(128)} %bitcast.me_ref, bf16[4,4,400,128]{3,2,1,0:T(8,128)(2,1)S(1)} %pad_maximum_fusion.parts_ref, f32[4,512,128]{2,1,0:T(8,128)S(1)} %get-tuple-element.20.carry_ref), custom_call_target="tpu_custom_call" | custom-call | tf_op jit(solution)/shard_map/spread/pallas_call | solution.py:548
  118.2 1.4 collective-permute-start.7
  120.1 13.5 %backward_maps.1.wx_ref = f32[256,4096]{1,0:T(8,128)} custom-call(bf16[256,2048]{1,0:T(8,128)(2,1)} %q_ref.5, bf16[256,2048]{1,0:T(8,128)(2,1)} %k_ref.5, bf16[256,2048]{1,0:T(8,128)(2,1)} %g_ref.5, bf16[256,2048]{1,0:T(8,128)(2,1)} %do_ref.5, bf16[256,16]{1,0:T(8,128)(2,1)} %copy.13.beta_ref, f32[256,4096]{1,0:T(8,128)} %get-tuple-element.14.ar_ref), custom_call_target="tpu_custom_call" | custom-call | flops 3221225472 | bytes 12582912 | tf_op jit(solution)/shard_map/backward_maps/pallas_call | solution.py:507
  133.6 1.2 pad_maximum_fusion.1.ends_ref
  134.8 26.6 %gradients.1 = (bf16[256,2048]{1,0:T(8,128)(2,1)}, bf16[256,2048]{1,0:T(8,128)(2,1)}, bf16[256,2048]{1,0:T(8,128)(2,1)}, bf16[256,2048]{1,0:T(8,128)(2,1)}, bf16[256,16]{1,0:T(8,128)(2,1)}) custom-call(s32[1]{0:T(128)} %bitcast.me_ref, bf16[256,2048]{1,0:T(8,128)(2,1)} %q_ref.5, bf16[256,2048]{1,0:T(8,128)(2,1)} %k_ref.5, bf16[256,2048]{1,0:T(8,128)(2,1)} %g_ref.5, ...), custom_call_target="tpu_custom_call" | custom-call | flops 6442450944 | bytes 20971520 | tf_op jit(solution)/shard_map/gradients/pallas_call | solution.py:559
  161.4 1.5 copy.14
  (17 shorter events, 2.6 us)
Async XLA Ops:
  42.0 12.3 %collective-permute-start.2 = (bf16[4,400,128]{2,1,0:T(8,128)(2,1)S(1)}, bf16[4,400,128]{2,1,0:T(8,128)(2,1)S(1)}, u32[]{:S(2)}, u32[]{:S(2)}) collective-permute-start(bf16[4,400,128]{2,1,0:T(8,128)(2,1)S(1)} %get-tuple-element.27), channel_id=1, source_target_pairs={{0,3},{1,2},{2,1},{3,0},{4,7},{5,6},{6,5},{7,4},{8,11},{9,10},{10,... | collective-permute-start | bytes 1228808 | tf_op jit(solution)/shard_map/ppermute | solution.py:500
  44.4 18.8 %collective-permute-start.1 = (bf16[4,400,128]{2,1,0:T(8,128)(2,1)S(1)}, bf16[4,400,128]{2,1,0:T(8,128)(2,1)S(1)}, u32[]{:S(2)}, u32[]{:S(2)}) collective-permute-start(bf16[4,400,128]{2,1,0:T(8,128)(2,1)S(1)} %get-tuple-element.28), channel_id=1, source_target_pairs={{0,2},{1,3},{2,0},{3,1},{4,6},{5,7},{6,4},{7,5},{8,10},{9,11},{10,... | collective-permute-start | bytes 1228808 | tf_op jit(solution)/shard_map/ppermute | solution.py:500
  45.1 18.1 %collective-permute-start = (bf16[4,400,128]{2,1,0:T(8,128)(2,1)S(1)}, bf16[4,400,128]{2,1,0:T(8,128)(2,1)S(1)}, u32[]{:S(2)}, u32[]{:S(2)}) collective-permute-start(bf16[4,400,128]{2,1,0:T(8,128)(2,1)S(1)} %get-tuple-element.29), channel_id=1, source_target_pairs={{0,1},{1,0},{2,3},{3,2},{4,5},{5,4},{6,7},{7,6},{8,9},{9,8},{10,11... | collective-permute-start | bytes 1228808 | tf_op jit(solution)/shard_map/ppermute | solution.py:500
  66.2 12.1 %collective-permute-start.3 = (bf16[4,400,128]{2,1,0:T(8,128)(2,1)S(1)}, bf16[4,400,128]{2,1,0:T(8,128)(2,1)S(1)}, u32[]{:S(2)}, u32[]{:S(2)}) collective-permute-start(bf16[4,400,128]{2,1,0:T(8,128)(2,1)S(1)} %compose.1.own_ref), channel_id=1, source_target_pairs={{0,4},{4,0},{8,12},{12,8},{16,20},{20,16},{24,28},{28,24},{1,5},{5... | collective-permute-start | bytes 1228808 | tf_op jit(solution)/shard_map/ppermute | solution.py:537
  78.8 1.0 copy-start
  79.8 10.9 %collective-permute-start.4 = (bf16[4,400,128]{2,1,0:T(8,128)(2,1)S(1)}, bf16[4,400,128]{2,1,0:T(8,128)(2,1)S(1)}, u32[]{:S(2)}, u32[]{:S(2)}) collective-permute-start(bf16[4,400,128]{2,1,0:T(8,128)(2,1)S(1)} %get-tuple-element.16.own_ref), channel_id=1, source_target_pairs={{0,8},{4,12},{8,0},{12,4},{16,24},{20,28},{24,16},{28,20},{1,9},{5... | collective-permute-start | bytes 1228808 | tf_op jit(solution)/shard_map/ppermute | solution.py:537
  90.7 0.8 copy-start.2
  91.4 1.2 copy-start.1
  92.6 1.0 copy-start.3
  94.2 19.7 %collective-permute-start.5 = (bf16[4,400,128]{2,1,0:T(8,128)(2,1)S(1)}, bf16[4,400,128]{2,1,0:T(8,128)(2,1)S(1)}, u32[]{:S(2)}, u32[]{:S(2)}) collective-permute-start(bf16[4,400,128]{2,1,0:T(8,128)(2,1)S(1)} %get-tuple-element.18.own_ref), channel_id=1, source_target_pairs={{0,16},{4,20},{8,24},{12,28},{16,0},{20,4},{24,8},{28,12},{1,17},{... | collective-permute-start | bytes 1228808 | tf_op jit(solution)/shard_map/ppermute | solution.py:537
  118.2 15.4 %collective-permute-start.8 = (bf16[4,256,128]{2,1,0:T(8,128)(2,1)S(1)}, bf16[4,256,128]{2,1,0:T(8,128)(2,1)S(1)}, u32[]{:S(2)}, u32[]{:S(2)}) collective-permute-start(bf16[4,256,128]{2,1,0:T(8,128)(2,1)S(1)} %get-tuple-element.31), channel_id=1, source_target_pairs={{0,3},{1,2},{2,1},{3,0},{4,7},{5,6},{6,5},{7,4},{8,11},{9,10},{10,... | collective-permute-start | bytes 786440 | tf_op jit(solution)/shard_map/ppermute | solution.py:500
  118.2 15.4 %collective-permute-start.7 = (bf16[4,256,128]{2,1,0:T(8,128)(2,1)S(1)}, bf16[4,256,128]{2,1,0:T(8,128)(2,1)S(1)}, u32[]{:S(2)}, u32[]{:S(2)}) collective-permute-start(bf16[4,256,128]{2,1,0:T(8,128)(2,1)S(1)} %get-tuple-element.32), channel_id=1, source_target_pairs={{0,2},{1,3},{2,0},{3,1},{4,6},{5,7},{6,4},{7,5},{8,10},{9,11},{10,... | collective-permute-start | bytes 786440 | tf_op jit(solution)/shard_map/ppermute | solution.py:500
  119.7 13.9 %collective-permute-start.6 = (bf16[4,256,128]{2,1,0:T(8,128)(2,1)S(1)}, bf16[4,256,128]{2,1,0:T(8,128)(2,1)S(1)}, u32[]{:S(2)}, u32[]{:S(2)}) collective-permute-start(bf16[4,256,128]{2,1,0:T(8,128)(2,1)S(1)} %get-tuple-element.33), channel_id=1, source_target_pairs={{0,1},{1,0},{2,3},{3,2},{4,5},{5,4},{6,7},{7,6},{8,9},{9,8},{10,11... | collective-permute-start | bytes 786440 | tf_op jit(solution)/shard_map/ppermute | solution.py:500

commit v2 on v1

v2 whole, which is shorter than its diff:
```python
import functools

import jax
import jax.numpy as jnp
import numpy as np
from jax import lax
from jax.experimental import pallas as pl
from jax.experimental.pallas import tpu as pltpu
from jax.sharding import PartitionSpec as P

DK = 128
DV = 128
SPAN = 128
STRIP = 16
ROWS = 3 * DK + 16
F32 = jnp.float32
BF16 = jnp.bfloat16


def split(x):
    if isinstance(x, tuple):
        return x
    if x.dtype == BF16:
        return (x, None)
    high = x.astype(BF16)
    return (high, (x - high.astype(F32)).astype(BF16))


def product(left, right, left_dim, right_dim, stacked=True):
    left_high, left_low = split(left)
    right_high, right_low = split(right)
    columns = right_high.shape[1 - right_dim]
    lefts, rights = [left_high], [right_high]
    wide = (
        left_low is not None
        and right_low is not None
        and columns <= DK
        and stacked
    )
    if wide:
        both = jnp.concatenate([right_high, right_low], axis=1 - right_dim)
        lefts, rights = [left_high, left_low], [both, both]
    else:
        if left_low is not None:
            lefts.append(left_low)
            rights.append(right_high)
        if right_low is not None:
            lefts.append(left_high)
            rights.append(right_low)
    left_all, right_all = lefts[0], rights[0]
    if len(lefts) > 1:
        left_all = jnp.concatenate(lefts, axis=left_dim)
        right_all = jnp.concatenate(rights, axis=right_dim)
    found = lax.dot_general(
        left_all, right_all, (((left_dim,), (right_dim,)), ((), ())), preferred_element_type=F32
    )
    return found[:, :columns] + found[:, columns:] if wide else found


def nn(left, right):
    return product(left, right, 1, 0)


def nt(left, right):
    return product(left, right, 1, 1)


def tn(left, right, stacked=False):
    return product(left, right, 0, 0, stacked)


def iotas(n=SPAN):
    return (
        lax.broadcasted_iota(jnp.int32, (n, n), 0),
        lax.broadcasted_iota(jnp.int32, (n, n), 1),
    )


def diagonal(row):
    rows, cols = iotas()
    return jnp.where(rows == cols, row, 0.0)


def column(row):
    return jnp.sum(diagonal(row), axis=1, keepdims=True)


def strip_map(fn, rows=SPAN):
    found = [fn(slice(i, i + STRIP)) for i in range(0, rows, STRIP)]
    return tuple(jnp.concatenate(parts, axis=0) for parts in zip(*found))


def split_strips(x):
    return strip_map(lambda at: split(x[at]), x.shape[0])


def level_masks():
    rows = np.arange(SPAN)[:, None]
    cols = np.arange(SPAN)[None, :]
    masks, size = [], 1
    while size < SPAN:
        masks.append((rows // size % 2 == 1) & (rows // size == cols // size + 1))
        size *= 2
    return jnp.asarray(np.stack(masks), BF16)


def unit_lower_inverses(strict, mask_ref):
    rows, cols = iotas()
    unit = jnp.where(rows == cols, 1.0, 0.0)
    mask = mask_ref[0].astype(F32)
    found = [strip_map(lambda at, n=n: whole_and_split(unit[at] - n[0][at] * mask[at])) for n in strict]
    strict = [(n[1], n[2]) for n in strict]
    for level in range(1, mask_ref.shape[0]):
        mask = mask_ref[level]
        inner = [split_strips(nn((n[0] * mask, n[1] * mask), x[1:])) for n, x in zip(strict, found)]
        outer = [nn(x[1:], i) for i, x in zip(inner, found)]
        found = [
            strip_map(lambda at, x=x, o=o: whole_and_split(x[0][at] - o[at])) for x, o in zip(found, outer)
        ]
    return [x[1:] for x in found]


def whole_and_split(x):
    return (x,) + split(x)


def decays(g):
    rows, cols = iotas()
    lower = jnp.where(rows >= cols, 1.0, 0.0).astype(BF16)
    running = nn(lower, g)
    middle = running[SPAN // 2 : SPAN // 2 + 1, :]
    ending = running[SPAN - 1 : SPAN, :]
    return running, middle, jnp.exp(middle), jnp.exp(ending - middle), jnp.exp(ending)


def head_betas(beta_ref, head):
    heads = beta_ref.shape[0]
    picked = jnp.where(
        lax.broadcasted_iota(jnp.int32, (heads, DK), 0) == head, 1.0, 0.0
    ).astype(BF16)
    return tn(beta_ref[...], picked)


class Side:
    def __init__(self, refs):
        self.refs, self.width = refs, refs[0].shape[1]
        self.shape = (refs[0].shape[0], self.width * len(refs))

    def __getitem__(self, at):
        rows, columns = at
        i = columns.start // self.width
        return self.refs[i][rows, columns.start - i * self.width : columns.stop - i * self.width]


def block_kernel(batch, groups, group, pair, me_ref, *refs):
    q_ref, k_ref, v_ref, g_ref, do_ref = [Side(refs[i * pair : (i + 1) * pair]) for i in range(5)]
    beta_ref, mask_ref, msg_ref, um_ref, ub_ref, ar_ref = refs[5 * pair :]
    swapped = jnp.bitwise_and(me_ref[0], pair - 1)
    first = pl.program_id(0) * pair
    own, batch = batch, pair * batch
    spans = q_ref.shape[0] // SPAN
    rows, cols = iotas()
    places = [(h, n) for h in range(batch) for n in range(spans)]
    betas = [
        head_betas(beta_ref, ((first + h // own) * groups + group) * own + h % own) for h in range(batch)
    ]
    tables, strict, reach, finals = {}, {}, {}, {}
    for h, n in places:
        base = n * SPAN
        wide = slice(h * DK, (h + 1) * DK)
        running, middle, start_factor, end_factor, final = decays(g_ref[base : base + SPAN, wide])
        finals[h, n] = final

        def table(at):
            of = slice(base + at.start, base + at.stop)
            up = jnp.exp(running[at] - middle)
            down = jnp.exp(middle - running[at])
            k = k_ref[of, wide].astype(F32)
            key_up = k * up
            query_up = q_ref[of, wide].astype(F32) * up
            write = k * down * betas[h][of]
            offset = query_up * start_factor
            return (
                split(key_up)
                + split(query_up)
                + split(write)
                + split(key_up * start_factor)
                + split(write * end_factor)
                + split(offset)
            )

        t = strip_map(table)
        tables[h, n] = dict(key_offset=t[6:8], key_end=t[8:10], query_offset=t[10:12])
        ups = (jnp.concatenate([t[0], t[2]], axis=0), jnp.concatenate([t[1], t[3]], axis=0))
        both = nt(ups, t[4:6])

        def scores(at):
            below = slice(at.start + SPAN, at.stop + SPAN)
            keys = jnp.where(rows[at] > cols[at], both[at], 0.0)
            queries = jnp.where(rows[at] >= cols[at], both[below], 0.0)
            return whole_and_split(keys) + split(queries)

        t = strip_map(scores)
        strict[h, n] = t[:3]
        reach[h, n] = t[3:]
    inverses = dict(zip(places, unit_lower_inverses([strict[p] for p in places], mask_ref)))
    solved = {}
    for h, n in places:
        of = slice(n * SPAN, (n + 1) * SPAN)
        base = h * 4 * SPAN
        for i, x in enumerate(inverses[h, n] + reach[h, n]):
            ar_ref[of, base + i * SPAN : base + (i + 1) * SPAN] = x
        solved[h, n] = (
            nn(inverses[h, n], tables[h, n]["key_offset"]),
            nn(inverses[h, n], v_ref[of, h * DK : (h + 1) * DK]),
        )
    state, read = {}, {}
    for n in range(spans):
        for h in range(batch):
            t = tables[h, n]
            across, value = solved[h, n]
            base = n * SPAN
            of = slice(base, base + SPAN)
            wide = slice(h * DK, (h + 1) * DK)
            if n == 0:
                ux_map = strip_map(lambda at: split(-across[at]))
                shift = value
            else:
                across = split_strips(across)
                moved = nn(across, (state[h][1], state[h][2]))
                ux_map = strip_map(lambda at: split(-moved[at, :DK]))
                (shift,) = strip_map(lambda at: (value[at] - moved[at, DK:],))
            ux_shift = split_strips(shift)
            ub_ref[of, wide] = shift
            um_ref[of, h * 2 * DK : h * 2 * DK + DK] = ux_map[0]
            um_ref[of, h * 2 * DK + DK : (h + 1) * 2 * DK] = ux_map[1]
            through = nn(reach[h, n], ux_map)
            if n == 0:
                direct = whole(t["query_offset"])
            else:
                direct = nn(t["query_offset"], (state[h][1][:, :DK], state[h][2][:, :DK]))
            out_map = strip_map(lambda at: split(direct[at] + through[at]))
            added = tn(
                t["key_end"],
                tuple(jnp.concatenate([m, s], axis=1) for m, s in zip(ux_map, ux_shift)),
            )
            if n == 0:
                kept = jnp.concatenate([diagonal(finals[h, n]), jnp.zeros((DK, DV), F32)], axis=1)
                (new,) = strip_map(lambda at: (kept[at] + added[at],))
            else:
                factor = column(finals[h, n])
                (new,) = strip_map(lambda at: (factor[at] * state[h][0][at] + added[at],))
            state[h] = (new,) + (split_strips(new) if n < spans - 1 else ())
            term = tn(out_map, do_ref[of, wide])
            read[h] = term if n == 0 else read[h] + term
    for h in range(batch):
        slot = (jnp.bitwise_xor(swapped, h // own), h % own)
        store_message(msg_ref, slot, state[h][0][:, :DK], state[h][0][:, DK:], read[h])


def store_message(msg_ref, place, block_map, shift, read):
    rows, cols = iotas()
    left = None
    for i in range(0, DK, STRIP):
        at = slice(i, i + STRIP)
        rounded = block_map[at].astype(BF16)
        msg_ref[*place, at, :] = rounded
        part = jnp.where(rows[at] == cols[at], block_map[at] - rounded.astype(F32), 0.0)
        left = part if left is None else left + part
        msg_ref[*place, DK + i : DK + i + STRIP, :] = shift[at].astype(BF16)
        msg_ref[*place, 2 * DK + i : 2 * DK + i + STRIP, :] = read[at].astype(BF16)
    msg_ref[*place, 3 * DK :, :] = jnp.broadcast_to(
        jnp.sum(left, axis=0, keepdims=True), (16, DK)
    ).astype(BF16)


def load_map(ref, *at):
    rows, cols = iotas()
    row = ref[at + (slice(3 * DK, ROWS), slice(None))][0:1, :].astype(F32)
    return (
        ref[at + (slice(0, DK), slice(None))],
        jnp.where(rows == cols, row, 0.0).astype(BF16),
    )


def load_shift(ref, *at):
    return ref[at + (slice(DK, 2 * DK), slice(None))]


def load_read(ref, *at):
    return ref[at + (slice(2 * DK, 3 * DK), slice(None))]


def whole_map(parts):
    return parts[0].astype(F32) + parts[1].astype(F32)


def backward_kernel(batch, groups, group, q_ref, k_ref, g_ref, do_ref, beta_ref, ar_ref, wm_ref, wb_ref):
    step = pl.program_id(0) * groups + group
    spans = q_ref.shape[0] // SPAN
    betas = [head_betas(beta_ref, step * batch + h) for h in range(batch)]
    carried = {}
    for n in range(spans - 1, -1, -1):
        for h in range(batch):
            base = n * SPAN
            of = slice(base, base + SPAN)
            wide = slice(h * DK, (h + 1) * DK)
            running, middle, start_factor, end_factor, final = decays(g_ref[of, wide])

            def table(at):
                of = slice(base + at.start, base + at.stop)
                k = k_ref[of, wide].astype(F32)
                found = split(k * jnp.exp(middle - running[at]) * betas[h][of] * end_factor)
                if n > 0:
                    up = jnp.exp(running[at] - middle) * start_factor
                    found += split(k * up) + split(q_ref[of, wide].astype(F32) * up)
                return found

            t = strip_map(table)
            do = do_ref[of, wide]
            inverse, reach = [
                tuple(
                    ar_ref[of, (h * 4 + i) * SPAN : (h * 4 + i + 1) * SPAN] for i in (j, j + 1)
                )
                for j in (0, 2)
            ]
            own = tn(inverse, split_strips(tn(reach, do)))
            through = split_strips(tn(inverse, t[0:2]))
            if n == spans - 1:
                wx_map, shift = through, own
            else:
                moved = nn(through, carried[h][1:])
                wx_map = strip_map(lambda at: split(moved[at, :DK]))
                (shift,) = strip_map(lambda at: (moved[at, DK:] + own[at],))
            wb_ref[of, wide] = shift
            wm_ref[of, h * 2 * DK : h * 2 * DK + DK] = wx_map[0]
            wm_ref[of, h * 2 * DK + DK : (h + 1) * 2 * DK] = wx_map[1]
            if n > 0:
                wx_shift = split_strips(shift)
                taken = tn(t[2:4], tuple(jnp.concatenate([m, s], axis=1) for m, s in zip(wx_map, wx_shift)))
                read = tn(t[4:6], do)
                if n == spans - 1:
                    kept = diagonal(final)
                    (left,) = strip_map(lambda at: (kept[at] - taken[at, :DK],))
                    (right,) = strip_map(lambda at: (read[at] - taken[at, DK:],))
                else:
                    factor = column(final)
                    before = carried[h][0]
                    (left,) = strip_map(lambda at: (factor[at] * before[at, :DK] - taken[at, :DK],))
                    (right,) = strip_map(
                        lambda at: (factor[at] * before[at, DK:] + read[at] - taken[at, DK:],)
                    )
                new = jnp.concatenate([left, right], axis=1)
                carried[h] = (new,) + split_strips(new)


def compose_kernel(me_ref, parts_ref, total_ref):
    me = me_ref[0]
    count, heads = parts_ref.shape[:2]
    states, reads = [], []
    for h in range(heads):
        first = load_map(parts_ref, me, h)
        states.append(jnp.concatenate([whole_map(first), load_shift(parts_ref, me, h).astype(F32)], axis=1))
        reads.append(load_read(parts_ref, jnp.bitwise_xor(me, count - 1), h).astype(F32))
    for j in range(1, count):
        at = jnp.bitwise_xor(me, j)
        back = jnp.bitwise_xor(me, count - 1 - j)
        for h in range(heads):
            moved = nn(load_map(parts_ref, at, h), states[h])
            states[h] = jnp.concatenate(
                [moved[:, :DK], moved[:, DK:] + load_shift(parts_ref, at, h).astype(F32)], axis=1
            )
            reads[h] = tn(load_map(parts_ref, back, h), reads[h]) + load_read(parts_ref, back, h).astype(F32)
    for h in range(heads):
        store_message(total_ref, (h,), states[h][:, :DK], states[h][:, DK:], reads[h])


def join_kernel(first, upper_ref, own_ref, other_ref, carry_ref, total_ref, next_ref):
    heads = own_ref.shape[0]
    rows, cols = iotas()
    unit = jnp.where(rows == cols, 1.0, 0.0)

    def part(i):
        return slice(i * DK, (i + 1) * DK)

    @pl.when(upper_ref[0] == 1)
    def _():
        for h in range(heads):
            early = load_map(other_ref, h)
            shift = load_shift(other_ref, h)
            if first:
                next_ref[h, part(0)] = whole_map(early)
                next_ref[h, part(1)] = shift.astype(F32)
                next_ref[h, part(2)] = jnp.zeros((DK, DV), F32)
                next_ref[h, part(3)] = unit
            else:
                before = split(carry_ref[h, part(0)])
                next_ref[h, part(0)] = nn(before, early)
                next_ref[h, part(1)] = nn(before, shift) + carry_ref[h, part(1)]
                next_ref[h, part(2)] = carry_ref[h, part(2)]
                next_ref[h, part(3)] = carry_ref[h, part(3)]
            late = load_map(own_ref, h)
            store_message(
                total_ref,
                (h,),
                nn(late, early),
                nn(late, shift) + load_shift(own_ref, h).astype(F32),
                load_read(other_ref, h).astype(F32) + tn(early, load_read(own_ref, h)),
            )

    @pl.when(upper_ref[0] == 0)
    def _():
        for h in range(heads):
            late = load_map(other_ref, h)
            read = load_read(other_ref, h)
            if first:
                next_ref[h, part(0)] = unit
                next_ref[h, part(1)] = jnp.zeros((DK, DV), F32)
                next_ref[h, part(2)] = read.astype(F32)
                next_ref[h, part(3)] = whole_map(late)
            else:
                after = split(carry_ref[h, part(3)])
                next_ref[h, part(0)] = carry_ref[h, part(0)]
                next_ref[h, part(1)] = carry_ref[h, part(1)]
                next_ref[h, part(2)] = tn(after, read) + carry_ref[h, part(2)]
                next_ref[h, part(3)] = nn(late, after)
            early = load_map(own_ref, h)
            store_message(
                total_ref,
                (h,),
                nn(late, early),
                nn(late, load_shift(own_ref, h)) + load_shift(other_ref, h).astype(F32),
                load_read(own_ref, h).astype(F32) + tn(early, read),
            )


def spread_kernel(me_ref, upper_ref, other_ref, parts_ref, carry_ref, out_ref, ends_ref):
    me = me_ref[0]
    count, heads = parts_ref.shape[:2]
    ends_ref[...] = carry_ref[:, DK : 3 * DK]

    @pl.when(upper_ref[0] == 1)
    def _():
        for h in range(heads):
            ends_ref[h, 0:DK] = carry_ref[h, DK : 2 * DK] + nn(carry_ref[h, 0:DK], other_ref[h])

    @pl.when(upper_ref[0] == 0)
    def _():
        for h in range(heads):
            ends_ref[h, DK:] = carry_ref[h, 2 * DK : 3 * DK] + tn(carry_ref[h, 3 * DK :], other_ref[h])

    states = [ends_ref[h, 0:DK] for h in range(heads)]
    grads = [ends_ref[h, DK:] for h in range(heads)]
    for j in range(count):
        at = jnp.bitwise_xor(me, j)
        back = jnp.bitwise_xor(me, count - 1 - j)
        for h in range(heads):
            out_ref[at, h, 0:DK] = states[h].astype(BF16)
            out_ref[back, h, DK:] = grads[h].astype(BF16)
            if j < count - 1:
                states[h] = nn(load_map(parts_ref, at, h), states[h]) + load_shift(parts_ref, at, h).astype(F32)
                grads[h] = tn(load_map(parts_ref, back, h), grads[h]) + load_read(parts_ref, back, h).astype(F32)


def gradient_kernel(
    batch, groups, group, me_ref, q_ref, k_ref, g_ref, do_ref, beta_ref, um_ref, ub_ref, wm_ref, wb_ref, ends_ref,
    *refs,
):
    del me_ref
    dq_ref, dk_ref, dv_ref, dg_ref, db_ref = refs[-5:]
    step = pl.program_id(0) * groups + group
    tokens = q_ref.shape[0]
    spans = tokens // SPAN
    rows, cols = iotas()
    upper = jnp.where(rows <= cols, 1.0, 0.0).astype(BF16)
    ones = jnp.ones((8, DV), BF16)
    heads = lax.broadcasted_iota(jnp.int32, (beta_ref.shape[0], tokens), 0)

    @pl.when(pl.program_id(0) == 0)
    def _():
        db_ref[...] = refs[0][...] if group else jnp.zeros_like(db_ref)

    all_gates = db_ref[...].astype(F32)
    for h in range(batch):
        head = step * batch + h
        beta = head_betas(beta_ref, head)
        wide = slice(h * DK, (h + 1) * DK)
        high_half = slice(h * 2 * DK, h * 2 * DK + DK)
        low_half = slice(h * 2 * DK + DK, (h + 1) * 2 * DK)
        start = ends_ref[h, 0:DK]
        end = ends_ref[h, DK:]
        moved = nn((um_ref[:, high_half], um_ref[:, low_half]), start)
        written = strip_map(lambda at: split(ub_ref[at, wide] + moved[at]), tokens)
        back = nn((wm_ref[:, high_half], wm_ref[:, low_half]), end)

        def writes(at):
            x = wb_ref[at, wide] + back[at]
            dv_ref[at, wide] = x.astype(BF16)
            return split(-x)

        left = strip_map(writes, tokens)
        sums, tables, us, lefts = [], [], [], []
        for n in range(spans):
            base = n * SPAN
            of = slice(base, base + SPAN)
            running, middle, start_factor, end_factor, final = decays(g_ref[of, wide])
            sums.append((running, middle, start_factor, end_factor, final))

            def table(at):
                of = slice(base + at.start, base + at.stop)
                up = jnp.exp(running[at] - middle)
                k = k_ref[of, wide].astype(F32)
                key_up = k * up
                query_up = q_ref[of, wide].astype(F32) * up
                write = k * jnp.exp(middle - running[at]) * beta[of]
                found = split(key_up) + split(query_up) + split(write)
                found += split(write * end_factor) if n < spans - 1 else (None, None)
                if n > 0:
                    found += split(key_up * start_factor) + split(query_up * start_factor)
                return found

            tables.append(optional_strips(table))
            us.append(tuple(x[of] for x in written))
            lefts.append(tuple(x[of] for x in left))
        states, grads = [start], [None] * spans
        state = start.astype(F32)
        for n in range(spans - 1):
            factor = column(sums[n][4])
            added = tn(tables[n][6:8], us[n], True)
            t = strip_map(lambda at: whole_and_split(factor[at] * state[at] + added[at]))
            state = t[0]
            states.append(t[1:])
        grads[spans - 1] = end
        grad = end.astype(F32)
        for n in range(spans - 1, 0, -1):
            factor = column(sums[n][4])
            added = tn(tables[n][8:10], lefts[n], True)
            read = tn(tables[n][10:12], do_ref[n * SPAN : (n + 1) * SPAN, wide])
            t = strip_map(lambda at: whole_and_split(factor[at] * grad[at] + added[at] + read[at]))
            grad = t[0]
            grads[n - 1] = t[1:]
        gates = []
        for n in range(spans):
            base = n * SPAN
            t = tables[n]
            high, low = lefts[n]
            do = do_ref[base : base + SPAN, wide]
            left = (
                jnp.concatenate([high, do], axis=0),
                jnp.concatenate([low, jnp.zeros_like(low)], axis=0),
            )
            held = states[n] if isinstance(states[n], tuple) else (states[n], jnp.zeros_like(states[n]))
            met = nt(left, tuple(jnp.concatenate(x, axis=0) for x in zip(held, us[n])))
            grad_end = nt(us[n], grads[n])

            def masked(at):
                below = slice(at.start + SPAN, at.stop + SPAN)
                keys = jnp.where(rows[at] > cols[at], met[at, DK:], 0.0)
                queries = jnp.where(rows[at] >= cols[at], met[below, DK:], 0.0)
                return split(keys) + split(queries)

            pairs = strip_map(masked)
            pairs = tuple(jnp.concatenate([pairs[i], pairs[i + 2]], axis=0) for i in range(2))
            raised = nn(pairs, t[4:6])
            ups = tuple(jnp.concatenate([t[i], t[i + 2]], axis=0) for i in range(2))
            downs = tn(pairs, ups, True)
            running, middle, start_factor, end_factor, final = sums[n]
            last = [None]

            def finish(at):
                of = slice(base + at.start, base + at.stop)
                up = jnp.exp(running[at] - middle)
                down = jnp.exp(middle - running[at])
                k = k_ref[of, wide].astype(F32)
                q = q_ref[of, wide].astype(F32)
                below = slice(at.start + SPAN, at.stop + SPAN)
                query_part = (raised[below] + met[below, :DK] * start_factor) * up
                key_part = (raised[at] + met[at, :DK] * start_factor) * up
                gate_part = (downs[at] + grad_end[at] * end_factor) * down
                write_part = gate_part * beta[of]
                dq_ref[of, wide] = query_part.astype(BF16)
                dk_ref[of, wide] = (key_part + write_part).astype(BF16)
                term = grad_end[at] * (k * down * beta[of])
                last[0] = term if last[0] is None else last[0] + term
                return split(q * query_part + k * (key_part - write_part)) + split(gate_part * k)

            flow_high, flow_low, *gate = strip_map(finish)
            gates.append(nt(ones, tuple(gate))[0:1])
            state, grad = states[n], grads[n]
            held = strip_map(lambda at: split(whole_at(state, at) * whole_at(grad, at)))
            row = jnp.sum(last[0], axis=0, keepdims=True) * end_factor + final * nt(ones, held)[0:1]
            sums_back = nn(upper, (flow_high, flow_low))
            for i in range(0, SPAN, STRIP):
                dg_ref[base + i : base + i + STRIP, wide] = (sums_back[i : i + STRIP] + row).astype(BF16)
        gate = jnp.concatenate(gates, axis=1)
        all_gates = jnp.where(heads == head, gate, all_gates)
    db_ref[...] = all_gates.astype(BF16)


def whole_at(x, at):
    if isinstance(x, tuple):
        return x[0][at].astype(F32) + x[1][at].astype(F32)
    return x[at].astype(F32)


def optional_strips(fn):
    found = [fn(slice(i, i + STRIP)) for i in range(0, SPAN, STRIP)]
    return tuple(
        None if parts[0] is None else jnp.concatenate(parts, axis=0) for parts in zip(*found)
    )


def whole(x):
    if isinstance(x, tuple):
        return x[0].astype(F32) + x[1].astype(F32)
    return x.astype(F32)


def params(semantics=("arbitrary",)):
    return pltpu.CompilerParams(dimension_semantics=semantics, vmem_limit_bytes=56 << 20)


def cost(flops, data):
    return pl.CostEstimate(flops=int(flops), bytes_accessed=int(data), transcendentals=0)


def exchange(parts, axis):
    count = parts.shape[0]
    return jnp.stack(
        [parts[0]]
        + [lax.ppermute(parts[d], axis, [(i, i ^ d) for i in range(count)]) for d in range(1, count)]
    )


SMEM = pl.BlockSpec(memory_space=pltpu.SMEM)
VMEM = pl.BlockSpec(memory_space=pltpu.VMEM)
SMALL = pltpu.CompilerParams(vmem_limit_bytes=40 << 20)


class Group:
    def __init__(self, tokens, heads, count, groups, group):
        self.tokens, self.heads, self.count = tokens, heads, count
        self.batch = heads // count // groups
        self.ids = (self.batch, groups, group)
        self.groups, self.group = groups, group
        self.flops = 2 * 3 * count * self.batch * tokens * DK * DK
        self.beta = pl.BlockSpec((heads, tokens), lambda i, *_: (0, 0))

    def paired(self, place, pair):
        return pl.BlockSpec(
            (self.tokens, self.batch * DK),
            lambda i, *_: (0, (i * pair + place) * self.groups + self.group),
        )

    def wide(self):
        return pl.BlockSpec(
            (self.tokens, self.batch * DK), lambda i, *_: (0, i * self.groups + self.group)
        )

    def own(self, columns):
        return pl.BlockSpec((self.tokens, self.batch * columns), lambda i, *_: (0, i))

    def ordered(self, rows):
        return pl.BlockSpec(
            (None, self.batch, rows, DK), lambda i, m: (jnp.bitwise_xor(i, m[0]), 0, 0, 0)
        )

    def tables(self, columns, kind):
        return jax.ShapeDtypeStruct((self.tokens, self.count * self.batch * columns), kind)

    def block_maps(self, me, queries, key_rows, value_matrix, log_decay, grad_out, beta_gate):
        masks = level_masks()
        pair = 2 if self.groups > 1 and self.count % 2 == 0 else 1
        arrays = (queries, key_rows, value_matrix, log_decay, grad_out)

        def own(columns):
            return pl.BlockSpec((self.tokens, pair * self.batch * columns), lambda i, *_: (0, i))

        return pl.pallas_call(
            functools.partial(block_kernel, *self.ids, pair),
            grid_spec=pltpu.PrefetchScalarGridSpec(
                num_scalar_prefetch=1,
                grid=(self.count // pair,),
                in_specs=[self.paired(place, pair) for _ in arrays for place in range(pair)]
                + [self.beta, pl.BlockSpec(masks.shape, lambda i, *_: (0, 0, 0))],
                out_specs=[
                    pl.BlockSpec(
                        (pair, self.batch, ROWS, DK),
                        lambda i, m: (jnp.bitwise_xor(i, m[0] // pair), 0, 0, 0),
                    ),
                    own(2 * DK),
                    own(DK),
                    own(4 * SPAN),
                ],
            ),
            out_shape=[
                jax.ShapeDtypeStruct((self.count, self.batch, ROWS, DK), BF16),
                self.tables(2 * DK, BF16),
                self.tables(DK, F32),
                self.tables(4 * SPAN, BF16),
            ],
            compiler_params=params(),
            cost_estimate=cost(24 * self.flops, 20 << 20),
            name="block_maps",
        )(me, *[x for x in arrays for _ in range(pair)], beta_gate, masks)

    def backward_maps(self, queries, key_rows, log_decay, grad_out, beta_gate, ar):
        return pl.pallas_call(
            functools.partial(backward_kernel, *self.ids),
            grid_spec=pltpu.PrefetchScalarGridSpec(
                num_scalar_prefetch=0,
                grid=(self.count,),
                in_specs=[self.wide()] * 4 + [self.beta, self.own(4 * SPAN)],
                out_specs=[self.own(2 * DK), self.own(DK)],
            ),
            out_shape=[self.tables(2 * DK, BF16), self.tables(DK, F32)],
            compiler_params=params(),
            cost_estimate=cost(8 * self.flops, 12 << 20),
            name="backward_maps",
        )(queries, key_rows, log_decay, grad_out, beta_gate, ar)

    def compose(self, me, parts):
        return pl.pallas_call(
            compose_kernel,
            in_specs=[SMEM, VMEM],
            out_specs=VMEM,
            out_shape=jax.ShapeDtypeStruct((self.batch, ROWS, DK), BF16),
            compiler_params=SMALL,
            name="compose",
        )(me, parts)

    def join(self, first, upper, total, other, carry):
        return pl.pallas_call(
            functools.partial(join_kernel, first),
            in_specs=[SMEM, VMEM, VMEM, VMEM],
            out_specs=[VMEM, VMEM],
            out_shape=[
                jax.ShapeDtypeStruct((self.batch, ROWS, DK), BF16),
                jax.ShapeDtypeStruct((self.batch, 4 * DK, DK), F32),
            ],
            compiler_params=SMALL,
            name="join",
        )(upper, total, other, carry)

    def spread(self, me, upper, other, parts, carry):
        return pl.pallas_call(
            spread_kernel,
            in_specs=[SMEM, SMEM, VMEM, VMEM, VMEM],
            out_specs=VMEM,
            out_shape=jax.ShapeDtypeStruct((self.count, self.batch, 2 * DK, DV), BF16),
            scratch_shapes=[pltpu.VMEM((self.batch, 2 * DK, DV), F32)],
            compiler_params=SMALL,
            name="spread",
        )(me, upper, other, parts, carry)

    def gradients(self, me, queries, key_rows, log_decay, grad_out, beta_gate, ux, wx, ends, before):
        inputs = [self.wide()] * 4 + [self.beta] + [self.own(2 * DK), self.own(DK)] * 2 + [self.ordered(2 * DK)]
        aliases = {}
        extra = ()
        if before is not None:
            inputs = inputs + [self.beta] + [pl.BlockSpec(memory_space=pl.ANY)] * 4
            aliases = {12 + i: i for i in range(4)}
            extra = (before[4],) + tuple(before[:4])
        token_shape = jax.ShapeDtypeStruct(queries.shape, BF16)
        return pl.pallas_call(
            functools.partial(gradient_kernel, *self.ids),
            grid_spec=pltpu.PrefetchScalarGridSpec(
                num_scalar_prefetch=1,
                grid=(self.count,),
                in_specs=inputs,
                out_specs=[self.wide()] * 4 + [self.beta],
            ),
            out_shape=[token_shape] * 4 + [jax.ShapeDtypeStruct(beta_gate.shape, BF16)],
            input_output_aliases=aliases,
            compiler_params=params(),
            cost_estimate=cost(16 * self.flops, 20 << 20),
            name="gradients",
        )(me, queries, key_rows, log_decay, grad_out, beta_gate, *ux, *wx, ends, *extra)


GROUPS = 2


def local(queries, key_rows, value_matrix, log_decay, beta_gate, grad_out):
    tokens, heads = beta_gate.shape
    beta_gate = beta_gate.T
    count = lax.axis_size("head")
    blocks = lax.axis_size("seq")
    me = lax.axis_index("head").astype(jnp.int32).reshape(1)
    place = lax.axis_index("seq").astype(jnp.int32)
    groups = GROUPS if (heads // count) % GROUPS == 0 else 1
    work = [Group(tokens, heads, count, groups, i) for i in range(groups)]
    ids = range(groups)

    def upper(distance):
        return (jnp.bitwise_and(place, distance) != 0).astype(jnp.int32).reshape(1)

    def swap(x, distance):
        return lax.ppermute(x, "seq", [(i, i ^ distance) for i in range(blocks)])

    tables = [
        w.block_maps(me, queries, key_rows, value_matrix, log_decay, grad_out, beta_gate) for w in work
    ]
    gathered = [exchange(tables[i][0], "head") for i in ids]
    wx = [
        w.backward_maps(queries, key_rows, log_decay, grad_out, beta_gate, tables[i][3])
        for i, w in enumerate(work)
    ]
    totals = [w.compose(me, gathered[i]) for i, w in enumerate(work)]
    carries = [jnp.zeros((w.batch, 4 * DK, DK), F32) for w in work]
    distance = 1
    while 2 * distance < blocks:
        for i, w in enumerate(work):
            totals[i], carries[i] = w.join(
                distance == 1, upper(distance), totals[i], swap(totals[i], distance), carries[i]
            )
        distance *= 2
    high = upper(distance)
    outs = None
    for i, w in enumerate(work):
        sent = jnp.where(high[0] == 1, totals[i][:, 2 * DK : 3 * DK], totals[i][:, DK : 2 * DK])
        ends = w.spread(me, high, swap(sent, distance), gathered[i], carries[i])
        ends = exchange(ends, "head")
        outs = w.gradients(
            me, queries, key_rows, log_decay, grad_out, beta_gate, tables[i][1:3], wx[i], ends, outs
        )
    return *outs[:4], outs[4].T


def solution(mesh):
    spec = P(("seq", "head"), None)
    return jax.shard_map(
        lambda *arrays: tuple(local(*arrays)),
        mesh=mesh,
        in_specs=(spec,) * 6,
        out_specs=(spec,) * 5,
        check_vma=False,
    )
```

time: 163 us -> 117 us (0.72)
  waiting for transfers between devices: 54 us -> 12.4 us
  starting transfers between devices: 11.8 us -> 19.9 us
  Pallas kernels: 86.5 us -> 78.8 us
  local copies, waits for them, and re-layouts: 8.5 us -> 2.69 us
    ppermute x9 -> x18, waiting for transfers between devices: 54 us -> 12.4 us  [the longest x12 8.28 us: exchange(): lax.ppermute(parts[d], axis, [(i, i ^ d) for i in range(count)])]
    ppermute x9 -> x18, starting transfers between devices: 11.8 us -> 19.9 us  [the longest x6 10.7 us: swap(): return lax.ppermute(x, 'seq', [(i, i ^ distance) for i in range(blocks)])]
    pallas_call x8 -> x14, Pallas kernels: 86.5 us -> 78.8 us  [the longest x2 29.5 us: gradients(): pl.pallas_call(functools.partial(gradient_kernel, *self.ids), grid_spec=p...]
    unnamed x9 -> x0, local copies, waits for them, and re-layouts: 5.36 us -> none
  transfers between devices with their start and end apart: 9 -> 18, of which waited for: 5 -> 4; matrix products, arithmetic and copies ran while one was open for 0% -> 2% of each run, Pallas kernels for 8% -> 30%
where the time goes in v2:
time: 117 us
  Pallas kernels  78.8 us (67%)
  starting transfers between devices  19.9 us (17%)
  waiting for transfers between devices  12.4 us (11%)
  local copies, waits for them, and re-layouts  2.69 us (2%)
  other arithmetic  2 us (2%)
    pallas_call x2, Pallas kernels, gradients(): pl.pallas_call(functools.partial(gradient_kernel, *self.ids), grid_spec=p...  29.5 us
    pallas_call x2, Pallas kernels, block_maps(): pl.pallas_call(functools.partial(block_kernel, *self.ids, pair), grid_spe...  27.8 us
    pallas_call x2, Pallas kernels, backward_maps(): pl.pallas_call(functools.partial(backward_kernel, *self.ids), grid_spec=p...  16 us
    ppermute x6, starting transfers between devices, swap(): return lax.ppermute(x, 'seq', [(i, i ^ distance) for i in range(blocks)])  10.7 us
    ppermute x12, starting transfers between devices, exchange(): lax.ppermute(parts[d], axis, [(i, i ^ d) for i in range(count)])  9.18 us
    ppermute x12, waiting for transfers between devices, exchange(): lax.ppermute(parts[d], axis, [(i, i ^ d) for i in range(count)])  8.28 us
    ppermute x6, waiting for transfers between devices, swap(): return lax.ppermute(x, 'seq', [(i, i ^ distance) for i in range(blocks)])  4.15 us
    slice x4, local copies, waits for them, and re-layouts, exchange(): parts[0]  2.66 us
  transfers between devices with their start and end apart: 18, of which 4 were waited for; matrix products, arithmetic and copies ran while one was open for 2% of the time, Pallas kernels for 30%

profile of v2, /device:TPU:0, one launch (start us, length us, event | category | flops | bytes accessed | tf_op | source)
XLA Modules:
  0.0 116.9 jit_solution(16699179709226853566)
XLA Ops:
  0.6 14.1 %block_maps.3 = (bf16[4,2,400,128]{3,2,1,0:T(8,128)(2,1)}, bf16[256,2048]{1,0:T(8,128)(2,1)}, f32[256,1024]{1,0:T(8,128)}, bf16[256,4096]{1,0:T(8,128)(2,1)}) custom-call(s32[1]{0:T(128)} %bitcast.me_ref, bf16[256,2048]{1,0:T(8,128)(2,1)} %q_ref.7, bf16[256,2048]{1,0:T(8,128)(2,1)} %q_ref.7, bf16[256,2048]{1,0:T(8,128)(2,1)} %k_ref.7, ...), custom_call_target="tpu_custom_call" | custom-call | flops 4831838208 | bytes 20971520 | tf_op jit(solution)/shard_map/block_maps/pallas_call | solution.py:679
  14.7 1.3 %fusion = (bf16[1,2,400,128]{3,2,1,0:T(8,128)(2,1)S(1)}, bf16[2,400,128]{2,1,0:T(8,128)(2,1)S(1)}, bf16[2,400,128]{2,1,0:T(8,128)(2,1)S(1)}, bf16[2,400,128]{2,1,0:T(8,128)(2,1)S(1)}) fusion(bf16[4,2,400,128]{3,2,1,0:T(8,128)(2,1)} %get-tuple-element.50), kind=kLoop, calls=%fused_computation.18 | loop fusion | bytes 1638400 | tf_op jit(solution)/shard_map/slice | solution.py:630
  16.0 2.4 %collective-permute-start.11 = (bf16[2,400,128]{2,1,0:T(8,128)(2,1)S(1)}, bf16[2,400,128]{2,1,0:T(8,128)(2,1)S(1)}, u32[]{:S(2)}, u32[]{:S(2)}) collective-permute-start(bf16[2,400,128]{2,1,0:T(8,128)(2,1)S(1)} %get-tuple-element.66), channel_id=1, source_target_pairs={{0,3},{1,2},{2,1},{3,0},{4,7},{5,6},{6,5},{7,4},{8,11},{9,10},{10,... | collective-permute-start | bytes 614408 | tf_op jit(solution)/shard_map/ppermute | solution.py:631
  19.1 13.7 %block_maps.2 = (bf16[4,2,400,128]{3,2,1,0:T(8,128)(2,1)}, bf16[256,2048]{1,0:T(8,128)(2,1)}, f32[256,1024]{1,0:T(8,128)}, bf16[256,4096]{1,0:T(8,128)(2,1)}) custom-call(s32[1]{0:T(128)} %bitcast.me_ref, bf16[256,2048]{1,0:T(8,128)(2,1)} %q_ref.7, bf16[256,2048]{1,0:T(8,128)(2,1)} %q_ref.7, bf16[256,2048]{1,0:T(8,128)(2,1)} %k_ref.7, ...), custom_call_target="tpu_custom_call" | custom-call | flops 4831838208 | bytes 20971520 | tf_op jit(solution)/shard_map/block_maps/pallas_call | solution.py:679
  32.8 1.3 %fusion.1 = (bf16[1,2,400,128]{3,2,1,0:T(8,128)(2,1)S(1)}, bf16[2,400,128]{2,1,0:T(8,128)(2,1)S(1)}, bf16[2,400,128]{2,1,0:T(8,128)(2,1)S(1)}, bf16[2,400,128]{2,1,0:T(8,128)(2,1)S(1)}) fusion(bf16[4,2,400,128]{3,2,1,0:T(8,128)(2,1)} %get-tuple-element.40), kind=kLoop, calls=%fused_computation.19 | loop fusion | bytes 1638400 | tf_op jit(solution)/shard_map/slice | solution.py:630
  34.1 1.5 %collective-permute-start.2 = (bf16[2,400,128]{2,1,0:T(8,128)(2,1)S(1)}, bf16[2,400,128]{2,1,0:T(8,128)(2,1)S(1)}, u32[]{:S(2)}, u32[]{:S(2)}) collective-permute-start(bf16[2,400,128]{2,1,0:T(8,128)(2,1)S(1)} %get-tuple-element.70), channel_id=1, source_target_pairs={{0,3},{1,2},{2,1},{3,0},{4,7},{5,6},{6,5},{7,4},{8,11},{9,10},{10,... | collective-permute-start | bytes 614408 | tf_op jit(solution)/shard_map/ppermute | solution.py:631
  37.2 1.6 %collective-permute-start.12 = (bf16[2,400,128]{2,1,0:T(8,128)(2,1)S(1)}, bf16[2,400,128]{2,1,0:T(8,128)(2,1)S(1)}, u32[]{:S(2)}, u32[]{:S(2)}) collective-permute-start(bf16[2,400,128]{2,1,0:T(8,128)(2,1)S(1)} %compose.3.own_ref), channel_id=1, source_target_pairs={{0,4},{4,0},{8,12},{12,8},{16,20},{20,16},{24,28},{28,24},{1,5},{5... | collective-permute-start | bytes 614408 | tf_op jit(solution)/shard_map/ppermute | solution.py:799
  38.8 2.3 %collective-permute-done.2 = bf16[2,400,128]{2,1,0:T(8,128)(2,1)S(1)} collective-permute-done((bf16[2,400,128]{2,1,0:T(8,128)(2,1)S(1)}, bf16[2,400,128]{2,1,0:T(8,128)(2,1)S(1)}, u32[]{:S(2)}, u32[]{:S(2)}) %collective-permute-start.2) | collective-permute-done | bytes 204832 | tf_op jit(solution)/shard_map/ppermute | solution.py:631
  41.1 4.8 %collective-permute-done.1 = bf16[2,400,128]{2,1,0:T(8,128)(2,1)S(1)} collective-permute-done((bf16[2,400,128]{2,1,0:T(8,128)(2,1)S(1)}, bf16[2,400,128]{2,1,0:T(8,128)(2,1)S(1)}, u32[]{:S(2)}, u32[]{:S(2)}) %collective-permute-start.1) | collective-permute-done | bytes 204832 | tf_op jit(solution)/shard_map/ppermute | solution.py:631
  46.9 1.9 %collective-permute-start.3 = (bf16[2,400,128]{2,1,0:T(8,128)(2,1)S(1)}, bf16[2,400,128]{2,1,0:T(8,128)(2,1)}, u32[]{:S(2)}, u32[]{:S(2)}) collective-permute-start(bf16[2,400,128]{2,1,0:T(8,128)(2,1)S(1)} %compose.2.own_ref), channel_id=1, source_target_pairs={{0,4},{4,0},{8,12},{12,8},{16,20},{20,16},{24,28},{28,24},{1,5},{5... | collective-permute-start | bytes 614408 | tf_op jit(solution)/shard_map/ppermute | solution.py:799
  49.0 1.6 %collective-permute-start.13 = (bf16[2,400,128]{2,1,0:T(8,128)(2,1)S(1)}, bf16[2,400,128]{2,1,0:T(8,128)(2,1)S(1)}, u32[]{:S(2)}, u32[]{:S(2)}) collective-permute-start(bf16[2,400,128]{2,1,0:T(8,128)(2,1)S(1)} %get-tuple-element.51.own_ref), channel_id=1, source_target_pairs={{0,8},{4,12},{8,0},{12,4},{16,24},{20,28},{24,16},{28,20},{1,9},{5... | collective-permute-start | bytes 614408 | tf_op jit(solution)/shard_map/ppermute | solution.py:799
  50.7 8.0 %backward_maps.3 = (bf16[256,2048]{1,0:T(8,128)(2,1)}, f32[256,1024]{1,0:T(8,128)}) custom-call(bf16[256,2048]{1,0:T(8,128)(2,1)} %q_ref.7, bf16[256,2048]{1,0:T(8,128)(2,1)} %k_ref.7, bf16[256,2048]{1,0:T(8,128)(2,1)} %g_ref.7, bf16[256,2048]{1,0:T(8,128)(2,1)} %do_ref.7, bf16[16,256]{1,0:T(8,128)(2,1)} %bitcast.56, bf16[256,4096]{1,0:T(8,128)(2,1)} %get-tuple-element.47.ar_ref), custom_call_target="tpu_custom_call" | custom-call | flops 1610612736 | bytes 12582912 | tf_op jit(solution)/shard_map/backward_maps/pallas_call | solution.py:708
  58.7 1.2 %join.4 = (bf16[2,400,128]{2,1,0:T(8,128)(2,1)S(1)}, f32[2,512,128]{2,1,0:T(8,128)S(1)}) custom-call(s32[1]{0:T(128)} %bitcast.4.upper_ref, bf16[2,400,128]{2,1,0:T(8,128)(2,1)S(1)} %compose.2.own_ref, bf16[2,400,128]{2,1,0:T(8,128)(2,1)} %collective-permute-done.3.other_ref, f32[2,512,128]{2,1,0:T(8,128)S(1)} %broadcast_1_carry_ref.2.carry_ref), custom_call_target="tpu_custom_call" | custom-call | tf_op jit(solution)/shard_map/join/pallas_call | solution.py:733
  60.8 2.7 %collective-permute-start.14 = (bf16[2,128,128]{2,1,0:T(8,128)(2,1)S(1)}, bf16[2,128,128]{2,1,0:T(8,128)(2,1)S(1)}, u32[]{:S(2)}, u32[]{:S(2)}) collective-permute-start(bf16[2,128,128]{2,1,0:T(8,128)(2,1)S(1)} %slice_select_fusion), channel_id=1, source_target_pairs={{0,16},{4,20},{8,24},{12,28},{16,0},{20,4},{24,8},{28,12},{1,17},{... | collective-permute-start | bytes 196616 | tf_op jit(solution)/shard_map/ppermute | solution.py:799
  63.5 4.1 %collective-permute-done.4.other_ref = bf16[2,400,128]{2,1,0:T(8,128)(2,1)S(1)} collective-permute-done((bf16[2,400,128]{2,1,0:T(8,128)(2,1)S(1)}, bf16[2,400,128]{2,1,0:T(8,128)(2,1)S(1)}, u32[]{:S(2)}, u32[]{:S(2)}) %collective-permute-start.4) | collective-permute-done | bytes 204832 | tf_op jit(solution)/shard_map/ppermute | solution.py:799
  68.0 2.5 %collective-permute-start.5 = (bf16[2,128,128]{2,1,0:T(8,128)(2,1)S(1)}, bf16[2,128,128]{2,1,0:T(8,128)(2,1)S(1)}, u32[]{:S(2)}, u32[]{:S(2)}) collective-permute-start(bf16[2,128,128]{2,1,0:T(8,128)(2,1)S(1)} %slice_select_fusion.1), channel_id=1, source_target_pairs={{0,16},{4,20},{8,24},{12,28},{16,0},{20,4},{24,8},{28,12},{1,17},{... | collective-permute-start | bytes 196616 | tf_op jit(solution)/shard_map/ppermute | solution.py:799
  70.4 0.9 spread.3
  71.5 1.5 %collective-permute-start.16 = (bf16[2,256,128]{2,1,0:T(8,128)(2,1)S(1)}, bf16[2,256,128]{2,1,0:T(8,128)(2,1)S(1)}, u32[]{:S(2)}, u32[]{:S(2)}) collective-permute-start(bf16[2,256,128]{2,1,0:T(8,128)(2,1)S(1)} %get-tuple-element.75), channel_id=1, source_target_pairs={{0,2},{1,3},{2,0},{3,1},{4,6},{5,7},{6,4},{7,5},{8,10},{9,11},{10,... | collective-permute-start | bytes 393224 | tf_op jit(solution)/shard_map/ppermute | solution.py:631
  73.3 0.9 spread.2
  74.2 1.1 collective-permute-start.8
  76.1 1.1 collective-permute-done.17
  77.3 8.1 %backward_maps.2 = (bf16[256,2048]{1,0:T(8,128)(2,1)}, f32[256,1024]{1,0:T(8,128)}) custom-call(bf16[256,2048]{1,0:T(8,128)(2,1)} %q_ref.7, bf16[256,2048]{1,0:T(8,128)(2,1)} %k_ref.7, bf16[256,2048]{1,0:T(8,128)(2,1)} %g_ref.7, bf16[256,2048]{1,0:T(8,128)(2,1)} %do_ref.7, bf16[16,256]{1,0:T(8,128)(2,1)} %bitcast.57, bf16[256,4096]{1,0:T(8,128)(2,1)} %get-tuple-element.37.ar_ref), custom_call_target="tpu_custom_call" | custom-call | flops 1610612736 | bytes 12582912 | tf_op jit(solution)/shard_map/backward_maps/pallas_call | solution.py:708
  87.2 14.7 %gradients.2 = (bf16[256,2048]{1,0:T(8,128)(2,1)}, bf16[256,2048]{1,0:T(8,128)(2,1)}, bf16[256,2048]{1,0:T(8,128)(2,1)}, bf16[256,2048]{1,0:T(8,128)(2,1)}, bf16[16,256]{1,0:T(8,128)(2,1)}) custom-call(s32[1]{0:T(128)} %bitcast.me_ref, bf16[256,2048]{1,0:T(8,128)(2,1)} %q_ref.7, bf16[256,2048]{1,0:T(8,128)(2,1)} %k_ref.7, bf16[256,2048]{1,0:T(8,128)(2,1)} %g_ref.7, ...), custom_call_target="tpu_custom_call" | custom-call | flops 3221225472 | bytes 20971520 | tf_op jit(solution)/shard_map/gradients/pallas_call | solution.py:765
  102.0 14.7 %gradients.3 = (bf16[256,2048]{1,0:T(8,128)(2,1)}, bf16[256,2048]{1,0:T(8,128)(2,1)}, bf16[256,2048]{1,0:T(8,128)(2,1)}, bf16[256,2048]{1,0:T(8,128)(2,1)}, bf16[16,256]{1,0:T(8,128)(2,1)}) custom-call(s32[1]{0:T(128)} %bitcast.me_ref, bf16[256,2048]{1,0:T(8,128)(2,1)} %q_ref.7, ...), custom_call_target="tpu_custom_call", output_to_operand_aliasing={{0}: (12, {}), {1}: (13, {}), {2}: (14, {}), {3}: (15, {})} | custom-call | flops 3221225472 | bytes 20971520 | tf_op jit(solution)/shard_map/gradients/pallas_call | solution.py:765
  (37 shorter events, 7.8 us)
Async XLA Ops:
  16.0 20.3 %collective-permute-start.11 = (bf16[2,400,128]{2,1,0:T(8,128)(2,1)S(1)}, bf16[2,400,128]{2,1,0:T(8,128)(2,1)S(1)}, u32[]{:S(2)}, u32[]{:S(2)}) collective-permute-start(bf16[2,400,128]{2,1,0:T(8,128)(2,1)S(1)} %get-tuple-element.66), channel_id=1, source_target_pairs={{0,3},{1,2},{2,1},{3,0},{4,7},{5,6},{6,5},{7,4},{8,11},{9,10},{10,... | collective-permute-start | bytes 614408 | tf_op jit(solution)/shard_map/ppermute | solution.py:631
  18.4 17.9 %collective-permute-start.10 = (bf16[2,400,128]{2,1,0:T(8,128)(2,1)S(1)}, bf16[2,400,128]{2,1,0:T(8,128)(2,1)S(1)}, u32[]{:S(2)}, u32[]{:S(2)}) collective-permute-start(bf16[2,400,128]{2,1,0:T(8,128)(2,1)S(1)} %get-tuple-element.67), channel_id=1, source_target_pairs={{0,2},{1,3},{2,0},{3,1},{4,6},{5,7},{6,4},{7,5},{8,10},{9,11},{10,... | collective-permute-start | bytes 614408 | tf_op jit(solution)/shard_map/ppermute | solution.py:631
  19.1 17.2 %collective-permute-start.9 = (bf16[2,400,128]{2,1,0:T(8,128)(2,1)S(1)}, bf16[2,400,128]{2,1,0:T(8,128)(2,1)S(1)}, u32[]{:S(2)}, u32[]{:S(2)}) collective-permute-start(bf16[2,400,128]{2,1,0:T(8,128)(2,1)S(1)} %get-tuple-element.68), channel_id=1, source_target_pairs={{0,1},{1,0},{2,3},{3,2},{4,5},{5,4},{6,7},{7,6},{8,9},{9,8},{10,11... | collective-permute-start | bytes 614408 | tf_op jit(solution)/shard_map/ppermute | solution.py:631
  34.1 7.0 %collective-permute-start.2 = (bf16[2,400,128]{2,1,0:T(8,128)(2,1)S(1)}, bf16[2,400,128]{2,1,0:T(8,128)(2,1)S(1)}, u32[]{:S(2)}, u32[]{:S(2)}) collective-permute-start(bf16[2,400,128]{2,1,0:T(8,128)(2,1)S(1)} %get-tuple-element.70), channel_id=1, source_target_pairs={{0,3},{1,2},{2,1},{3,0},{4,7},{5,6},{6,5},{7,4},{8,11},{9,10},{10,... | collective-permute-start | bytes 614408 | tf_op jit(solution)/shard_map/ppermute | solution.py:631
  35.7 10.3 %collective-permute-start.1 = (bf16[2,400,128]{2,1,0:T(8,128)(2,1)S(1)}, bf16[2,400,128]{2,1,0:T(8,128)(2,1)S(1)}, u32[]{:S(2)}, u32[]{:S(2)}) collective-permute-start(bf16[2,400,128]{2,1,0:T(8,128)(2,1)S(1)} %get-tuple-element.71), channel_id=1, source_target_pairs={{0,2},{1,3},{2,0},{3,1},{4,6},{5,7},{6,4},{7,5},{8,10},{9,11},{10,... | collective-permute-start | bytes 614408 | tf_op jit(solution)/shard_map/ppermute | solution.py:631
  36.3 9.7 %collective-permute-start = (bf16[2,400,128]{2,1,0:T(8,128)(2,1)S(1)}, bf16[2,400,128]{2,1,0:T(8,128)(2,1)S(1)}, u32[]{:S(2)}, u32[]{:S(2)}) collective-permute-start(bf16[2,400,128]{2,1,0:T(8,128)(2,1)S(1)} %get-tuple-element.72), channel_id=1, source_target_pairs={{0,1},{1,0},{2,3},{3,2},{4,5},{5,4},{6,7},{7,6},{8,9},{9,8},{10,11... | collective-permute-start | bytes 614408 | tf_op jit(solution)/shard_map/ppermute | solution.py:631
  37.2 11.5 %collective-permute-start.12 = (bf16[2,400,128]{2,1,0:T(8,128)(2,1)S(1)}, bf16[2,400,128]{2,1,0:T(8,128)(2,1)S(1)}, u32[]{:S(2)}, u32[]{:S(2)}) collective-permute-start(bf16[2,400,128]{2,1,0:T(8,128)(2,1)S(1)} %compose.3.own_ref), channel_id=1, source_target_pairs={{0,4},{4,0},{8,12},{12,8},{16,20},{20,16},{24,28},{28,24},{1,5},{5... | collective-permute-start | bytes 614408 | tf_op jit(solution)/shard_map/ppermute | solution.py:799
  46.9 11.8 %collective-permute-start.3 = (bf16[2,400,128]{2,1,0:T(8,128)(2,1)S(1)}, bf16[2,400,128]{2,1,0:T(8,128)(2,1)}, u32[]{:S(2)}, u32[]{:S(2)}) collective-permute-start(bf16[2,400,128]{2,1,0:T(8,128)(2,1)S(1)} %compose.2.own_ref), channel_id=1, source_target_pairs={{0,4},{4,0},{8,12},{12,8},{16,20},{20,16},{24,28},{28,24},{1,5},{5... | collective-permute-start | bytes 614408 | tf_op jit(solution)/shard_map/ppermute | solution.py:799
  49.0 11.4 %collective-permute-start.13 = (bf16[2,400,128]{2,1,0:T(8,128)(2,1)S(1)}, bf16[2,400,128]{2,1,0:T(8,128)(2,1)S(1)}, u32[]{:S(2)}, u32[]{:S(2)}) collective-permute-start(bf16[2,400,128]{2,1,0:T(8,128)(2,1)S(1)} %get-tuple-element.51.own_ref), channel_id=1, source_target_pairs={{0,8},{4,12},{8,0},{12,4},{16,24},{20,28},{24,16},{28,20},{1,9},{5... | collective-permute-start | bytes 614408 | tf_op jit(solution)/shard_map/ppermute | solution.py:799
  59.9 7.7 %collective-permute-start.4 = (bf16[2,400,128]{2,1,0:T(8,128)(2,1)S(1)}, bf16[2,400,128]{2,1,0:T(8,128)(2,1)S(1)}, u32[]{:S(2)}, u32[]{:S(2)}) collective-permute-start(bf16[2,400,128]{2,1,0:T(8,128)(2,1)S(1)} %get-tuple-element.41.own_ref), channel_id=1, source_target_pairs={{0,8},{4,12},{8,0},{12,4},{16,24},{20,28},{24,16},{28,20},{1,9},{5... | collective-permute-start | bytes 614408 | tf_op jit(solution)/shard_map/ppermute | solution.py:799
  60.8 9.6 %collective-permute-start.14 = (bf16[2,128,128]{2,1,0:T(8,128)(2,1)S(1)}, bf16[2,128,128]{2,1,0:T(8,128)(2,1)S(1)}, u32[]{:S(2)}, u32[]{:S(2)}) collective-permute-start(bf16[2,128,128]{2,1,0:T(8,128)(2,1)S(1)} %slice_select_fusion), channel_id=1, source_target_pairs={{0,16},{4,20},{8,24},{12,28},{16,0},{20,4},{24,8},{28,12},{1,17},{... | collective-permute-start | bytes 196616 | tf_op jit(solution)/shard_map/ppermute | solution.py:799
  68.0 5.3 %collective-permute-start.5 = (bf16[2,128,128]{2,1,0:T(8,128)(2,1)S(1)}, bf16[2,128,128]{2,1,0:T(8,128)(2,1)S(1)}, u32[]{:S(2)}, u32[]{:S(2)}) collective-permute-start(bf16[2,128,128]{2,1,0:T(8,128)(2,1)S(1)} %slice_select_fusion.1), channel_id=1, source_target_pairs={{0,16},{4,20},{8,24},{12,28},{16,0},{20,4},{24,8},{28,12},{1,17},{... | collective-permute-start | bytes 196616 | tf_op jit(solution)/shard_map/ppermute | solution.py:799
  71.4 5.9 %collective-permute-start.17 = (bf16[2,256,128]{2,1,0:T(8,128)(2,1)S(1)}, bf16[2,256,128]{2,1,0:T(8,128)(2,1)S(1)}, u32[]{:S(2)}, u32[]{:S(2)}) collective-permute-start(bf16[2,256,128]{2,1,0:T(8,128)(2,1)S(1)} %get-tuple-element.74), channel_id=1, source_target_pairs={{0,3},{1,2},{2,1},{3,0},{4,7},{5,6},{6,5},{7,4},{8,11},{9,10},{10,... | collective-permute-start | bytes 393224 | tf_op jit(solution)/shard_map/ppermute | solution.py:631
  71.5 14.0 %collective-permute-start.16 = (bf16[2,256,128]{2,1,0:T(8,128)(2,1)S(1)}, bf16[2,256,128]{2,1,0:T(8,128)(2,1)S(1)}, u32[]{:S(2)}, u32[]{:S(2)}) collective-permute-start(bf16[2,256,128]{2,1,0:T(8,128)(2,1)S(1)} %get-tuple-element.75), channel_id=1, source_target_pairs={{0,2},{1,3},{2,0},{3,1},{4,6},{5,7},{6,4},{7,5},{8,10},{9,11},{10,... | collective-permute-start | bytes 393224 | tf_op jit(solution)/shard_map/ppermute | solution.py:631
  73.0 12.5 %collective-permute-start.15 = (bf16[2,256,128]{2,1,0:T(8,128)(2,1)S(1)}, bf16[2,256,128]{2,1,0:T(8,128)(2,1)S(1)}, u32[]{:S(2)}, u32[]{:S(2)}) collective-permute-start(bf16[2,256,128]{2,1,0:T(8,128)(2,1)S(1)} %get-tuple-element.76), channel_id=1, source_target_pairs={{0,1},{1,0},{2,3},{3,2},{4,5},{5,4},{6,7},{7,6},{8,9},{9,8},{10,11... | collective-permute-start | bytes 393224 | tf_op jit(solution)/shard_map/ppermute | solution.py:631
  74.2 12.1 %collective-permute-start.8 = (bf16[2,256,128]{2,1,0:T(8,128)(2,1)S(1)}, bf16[2,256,128]{2,1,0:T(8,128)(2,1)S(1)}, u32[]{:S(2)}, u32[]{:S(2)}) collective-permute-start(bf16[2,256,128]{2,1,0:T(8,128)(2,1)S(1)} %get-tuple-element.78), channel_id=1, source_target_pairs={{0,3},{1,2},{2,1},{3,0},{4,7},{5,6},{6,5},{7,4},{8,11},{9,10},{10,... | collective-permute-start | bytes 393224 | tf_op jit(solution)/shard_map/ppermute | solution.py:631
  75.4 11.0 %collective-permute-start.7 = (bf16[2,256,128]{2,1,0:T(8,128)(2,1)S(1)}, bf16[2,256,128]{2,1,0:T(8,128)(2,1)S(1)}, u32[]{:S(2)}, u32[]{:S(2)}) collective-permute-start(bf16[2,256,128]{2,1,0:T(8,128)(2,1)S(1)} %get-tuple-element.79), channel_id=1, source_target_pairs={{0,2},{1,3},{2,0},{3,1},{4,6},{5,7},{6,4},{7,5},{8,10},{9,11},{10,... | collective-permute-start | bytes 393224 | tf_op jit(solution)/shard_map/ppermute | solution.py:631
  77.2 9.1 %collective-permute-start.6 = (bf16[2,256,128]{2,1,0:T(8,128)(2,1)S(1)}, bf16[2,256,128]{2,1,0:T(8,128)(2,1)S(1)}, u32[]{:S(2)}, u32[]{:S(2)}) collective-permute-start(bf16[2,256,128]{2,1,0:T(8,128)(2,1)S(1)} %get-tuple-element.80), channel_id=1, source_target_pairs={{0,1},{1,0},{2,3},{3,2},{4,5},{5,4},{6,7},{7,6},{8,9},{9,8},{10,11... | collective-permute-start | bytes 393224 | tf_op jit(solution)/shard_map/ppermute | solution.py:631
